TPU v7x, 128 devices: a whole 4x4x4 slice. The times are simulated.
128 devices in a mesh: row: 16 (over z, y), col: 8 (over x, core).
Axes of the slice: x: 4, y: 4, z: 4, core: 2. Of those that a mesh axis runs over, the one named last changes fastest.
Arguments:
- activations: bfloat16 [32768, 4096], P(('row', 'col')), may hold values from -6 to 6
- out_grads: bfloat16 [32768, 4096], P(('row', 'col')), may hold values from -6 to 6
- proj_in: bfloat16 [4096, 128], replicated, may hold values from -0.09375 to 0.09375
- proj_out: bfloat16 [4096, 128], replicated, may hold values from -0.09375 to 0.09375
- lengths: int32 [1024], P(('row', 'col')), may hold values from 1 to 32, 24576 in all
- gram_old: float32 [16384, 16384], P('row', 'col'), as said below
- queries: float32 [16384, 256], P('row'), may hold values from -96 to 96
Outputs:
- gram_new: float32 [16384, 16384], P('row', 'col')
- solution: float32 [16384, 256], P('row')
Inputs may be any that keep to these rules, and one draw needn't show every extreme that they name: `gram_old`: symmetric and positive definite. Example e's token slots from lengths[e] on are padding.
All inputs are finite; a program needn't handle non-finite values. No bound on the sum of `lengths` on one device may be relied on, other than what follows from the above.
Results may differ from a plain program's by a relative error of at most 0.0055.
Values may be sent and summed in bfloat16 or wider, within the bound.
A program may use at most 192 MiB of HBM per device.

v0:
```python
import jax
import jax.numpy as jnp
from jax import lax
from jax.sharding import PartitionSpec as P

SEQ = 32
ITERS = 2


decay_rate = 0.5
damping = 1.0


def spread(value, axis, root):
    mine = lax.axis_index(axis) == root
    return lax.psum(jnp.where(mine, value, jnp.zeros_like(value)), axis)


def over_pieces(value, axis):
    blocks = lax.all_gather(value, axis)
    return blocks.sum(axis=0)


def from_everyone(value, axis):
    peers = lax.axis_size(axis)
    return lax.all_to_all(
        jnp.broadcast_to(value[None], (peers, *value.shape)), axis, 0, 0, tiled=True
    )


def taken_together(value, axis):
    everything = from_everyone(value, axis)
    return jnp.sum(everything, axis=0)


def in_one(arrays, axis):
    ends = [0]
    for a in arrays:
        ends.append(ends[-1] + a.size)
    total = taken_together(jnp.concatenate([a.ravel() for a in arrays]), axis)
    return tuple((total[b:e].reshape(a.shape) for a, b, e in zip(arrays, ends, ends[1:])))


def shards(activations, out_grads, proj_in, proj_out, lengths, gram_old, queries):
    local_count = lengths.shape[0]
    proj_rank = proj_in.shape[1]
    features = proj_rank * proj_rank
    row_count = lax.axis_size("row")
    col_count = lax.axis_size("col")
    row_block = gram_old.shape[0]
    col_block = gram_old.shape[1]
    row_start = lax.axis_index("row") * row_block
    col_start = lax.axis_index("col") * col_block
    low_in = jnp.dot(activations, proj_in, preferred_element_type=jnp.float32).astype(jnp.bfloat16)
    low_out = jnp.dot(out_grads, proj_out, preferred_element_type=jnp.float32).astype(jnp.bfloat16)
    low_in = low_in.reshape(local_count, SEQ, proj_rank)
    low_out = low_out.reshape(local_count, SEQ, proj_rank)
    valid_mask = jnp.arange(SEQ)[None, :] < lengths[:, None]
    low_out = jnp.where(valid_mask[:, :, None], low_out, jnp.zeros((), jnp.bfloat16))
    local_grads = jnp.einsum(
        "eto,eti->eoi", low_out.astype(jnp.float32), low_in.astype(jnp.float32)
    )
    local_grads = local_grads.reshape(local_count, features).astype(jnp.bfloat16)
    shard_rows = lax.all_gather(local_grads, ("row", "col"), axis=0, tiled=True)
    left_part = lax.dynamic_slice_in_dim(shard_rows, row_start, row_block, 1)
    right_part = lax.dynamic_slice_in_dim(shard_rows, col_start, col_block, 1)
    product = lax.dot_general(
        left_part, right_part, (((0,), (0,)), ((), ())), preferred_element_type=jnp.float32
    )
    total_examples = local_count * row_count * col_count
    gram_new = decay_rate * gram_old + (1.0 - decay_rate) / total_examples * product
    rows_global = row_start + jnp.arange(row_block, dtype=jnp.int32)
    cols_global = col_start + jnp.arange(col_block, dtype=jnp.int32)
    gram_new = gram_new + jnp.where(
        rows_global[:, None] == cols_global[None, :], damping, 0.0
    ).astype(jnp.float32)

    def operate(vector_block):
        blocks_per_col = row_count // col_count
        members = []
        for member in range(blocks_per_col):
            members.append(
                spread(vector_block, "row", blocks_per_col * lax.axis_index("col") + member)
            )
        col_part = jnp.concatenate(members, 0)
        partial_value = jnp.dot(
            gram_new, col_part, precision=lax.Precision.HIGHEST, preferred_element_type=jnp.float32
        )
        return over_pieces(partial_value, "col")

    def paired_sums(residual, mapped):
        return in_one(
            (jnp.sum(residual * residual, axis=0), jnp.sum(residual * mapped, axis=0)), "row"
        )

    solution = jnp.zeros_like(queries)
    residual = queries
    mapped = operate(residual)
    norm_now, curvature_sum = paired_sums(residual, mapped)
    step_size = norm_now / curvature_sum
    direction = residual
    along = mapped
    for sweep in range(ITERS):
        solution = solution + step_size * direction
        if sweep + 1 < ITERS:
            residual = residual - step_size * along
            mapped = operate(residual)
            norm_next, curvature_sum = paired_sums(residual, mapped)
            momentum = norm_next / norm_now
            step_size = norm_next / (curvature_sum - momentum * norm_next / step_size)
            direction = residual + momentum * direction
            along = mapped + momentum * along
            norm_now = norm_next
    return (gram_new, solution)


def solution(mesh):
    in_specs = (
        P(("row", "col"), None),
        P(("row", "col"), None),
        P(),
        P(),
        P(("row", "col")),
        P("row", "col"),
        P("row", None),
    )
    out_specs = (P("row", "col"), P("row", None))
    return jax.shard_map(shards, mesh=mesh, in_specs=in_specs, out_specs=out_specs, check_vma=False)
```

profile of v0, /device:TPU:1, one launch (start us, length us, event | category | flops | bytes accessed | tf_op | source)
XLA Modules:
  0.0 408.6 jit_solution(14874443476713835550)
XLA Ops:
  8.0 0.0 copy-start
  8.0 0.0 all-gather.6.cloned.1.call-start
  8.1 0.9 iota_compare_fusion
  8.9 0.7 copy-done
  9.6 1.9 convolution_convert_fusion.1
  11.5 2.6 convolution_convert_fusion.2
  14.1 0.3 fusion.10
  14.4 0.9 copy.19
  15.3 0.0 all-gather.6.cloned.1.call-update
  15.3 0.0 all-reduce.7.cloned.1.call-start
  15.4 2.7 broadcast_select_fusion.3
  18.1 0.0 all-reduce.7.cloned.1.call-update
  18.1 0.0 all-gather.8.cloned.1.call-start
  18.2 111.1 %all-gather.6.cloned.1.call-done = bf16[1024,16384]{1,0:T(8,128)(2,1)} async-done(((bf16[8,16384]{1,0:T(8,128)(2,1)}), bf16[1024,16384]{1,0:T(8,128)(2,1)}) %all-gather.6.cloned.1.call-update) | async-done | bytes 33554448 | tf_op jit(solution)/shard_map/all_gather | solution.py:64
  129.4 14.2 %select_add_fusion = f32[1024,2048]{1,0:T(8,128)} fusion(f32[1024,2048]{1,0:T(8,128)} %param.12, s32[2048]{0:T(1024)S(1)} %iota_add_fusion, bf16[1024,16384]{1,0:T(8,128)(2,1)} %all-gather.6.cloned.1.call-done, s32[]{:T(128)S(6)} %select_n.38, s32[1024]{0:T(1024)S(1)} %iota_add_fusion.1, s32[]{:T(128)S(6)} %select_n.37), kind=kOutput, calls=%fused_computation | convolution fusion | flops 4307550208 | bytes 23080968 | tf_op jit(solution)/shard_map/dot_general | solution.py:67
  143.6 6.1 %all-reduce.7.cloned.1.call-done = (f32[1024,256]{1,0:T(8,128)}, f32[1024,256]{1,0:T(8,128)}) async-done(((f32[1024,256]{1,0:T(8,128)}, f32[1024,256]{1,0:T(8,128)}), (f32[1024,256]{1,0:T(8,128)}, f32[1024,256]{1,0:T(8,128)})) %all-reduce.7.cloned.1.call-update) | async-done | bytes 2097168 | tf_op jit(solution)/shard_map/psum | solution.py:16
  149.6 10.5 %fusion.1 = f32[1024,256]{1,0:T(8,128)} fusion(f32[1024,2048]{1,0:T(8,128)} %select_add_fusion, f32[1024,256]{1,0:T(8,128)} %get-tuple-element.8, f32[1024,256]{1,0:T(8,128)} %get-tuple-element.9), kind=kOutput, calls=%fused_computation.2 | convolution fusion | flops 6442975232 | bytes 11534336 | tf_op jit(solution)/shard_map/dot_general | solution.py:86
  160.1 0.0 copy-start.2
  160.1 0.0 all-gather.8.cloned.1.call-update
  160.2 0.2 all-reduce.5.cloned.1.call-start
  160.4 50.7 %all-gather.8.cloned.1.call-done = f32[8192,256]{1,0:T(8,128)} async-done(((f32[1024,256]{1,0:T(8,128)}), f32[8192,256]{1,0:T(8,128)}) %all-gather.8.cloned.1.call-update) | async-done | bytes 8388624 | tf_op jit(solution)/shard_map/all_gather | solution.py:20
  211.1 4.1 reduce_sum.73
  215.1 0.0 copy-done.2
  215.2 0.2 multiply_reduce_fusion.3
  215.4 13.0 %all_to_all.12 = f32[16,1,512]{2,1,0:T(1,128)S(1)} all-to-all(f32[16,1,512]{2,1,0:T(1,128)S(1)} %broadcast_in_dim.28), channel_id=1, replica_groups=mesh['row'=16,'col'=8] {'row'}, dimensions={0} | all-to-all | bytes 65536 | tf_op jit(solution)/shard_map/all_to_all | solution.py:26
  228.4 1.2 broadcast_select_fusion.1
  229.6 1.1 broadcast_select_fusion
  230.6 0.0 all-reduce.5.cloned.1.call-update
  230.7 0.0 all-gather.10.cloned.1.call-start
  230.7 86.8 %all-reduce.5.cloned.1.call-done = (f32[1024,256]{1,0:T(8,128)}, f32[1024,256]{1,0:T(8,128)}) async-done(((f32[1024,256]{1,0:T(8,128)}, f32[1024,256]{1,0:T(8,128)}), (f32[1024,256]{1,0:T(8,128)}, f32[1024,256]{1,0:T(8,128)})) %all-reduce.5.cloned.1.call-update) | async-done | bytes 2097168 | tf_op jit(solution)/shard_map/psum | solution.py:16
  317.6 0.0 copy-start.1
  317.6 10.6 %fusion.5 = f32[1024,256]{1,0:T(8,128)} fusion(f32[1024,2048]{1,0:T(8,128)} %select_add_fusion, f32[1024,256]{1,0:T(8,128)} %get-tuple-element.6, f32[1024,256]{1,0:T(8,128)} %get-tuple-element.7), kind=kOutput, calls=%fused_computation.6 | convolution fusion | flops 6442975232 | bytes 11534336 | tf_op jit(solution)/shard_map/dot_general | solution.py:86
  328.2 0.0 all-gather.10.cloned.1.call-update
  328.2 50.9 %all-gather.10.cloned.1.call-done = f32[8192,256]{1,0:T(8,128)} async-done(((f32[1024,256]{1,0:T(8,128)}), f32[8192,256]{1,0:T(8,128)}) %all-gather.10.cloned.1.call-update) | async-done | bytes 8388624 | tf_op jit(solution)/shard_map/all_gather | solution.py:20
  379.1 5.0 %reduce_sum.77 = f32[1024,256]{1,0:T(8,128)} reduce(f32[8,1024,256]{2,1,0:T(8,128)} %bitcast.17, f32[]{:T(128)} %constant.13.clone.1), dimensions={0}, to_apply=%region_9.10 | reduce | flops 1835008 | bytes 9437188 | tf_op jit(solution)/shard_map/reduce_sum | solution.py:21
  384.2 1.4 multiply_reduce_fusion.1
  385.6 13.0 %all_to_all.13 = f32[16,1,512]{2,1,0:T(1,128)S(1)} all-to-all(f32[16,1,512]{2,1,0:T(1,128)S(1)} %broadcast_in_dim.46), channel_id=1, replica_groups=mesh['row'=16,'col'=8] {'row'}, dimensions={0} | all-to-all | bytes 65536 | tf_op jit(solution)/shard_map/all_to_all | solution.py:26
  398.6 2.4 multiply_add_fusion
  401.0 0.0 copy-done.1
  (10 shorter events, 0.2 us)
Async XLA Ops:
  8.0 1.6 copy-start
  8.0 121.3 %all-gather.6.cloned.1.call-start = ((), (), s32[]{:S(2)}) async-start(), calls=%async_computation.2 | async-start | bytes 33816576 | tf_op jit(solution)/shard_map/all_gather | solution.py:64
  15.3 134.3 %all-reduce.7.cloned.1.call-start = ((), (), s32[]{:S(2)}) async-start(), calls=%async_computation.6 | async-start | bytes 4194304 | tf_op jit(solution)/shard_map/psum | solution.py:16
  18.1 193.0 %all-gather.8.cloned.1.call-start = ((), (), s32[]{:S(2)}) async-start(), calls=%async_computation.3 | async-start | bytes 9437184 | tf_op jit(solution)/shard_map/all_gather | solution.py:20
  160.1 55.0 %copy-start.2 = (f32[1024,256]{1,0:T(8,128)S(1)}, f32[1024,256]{1,0:T(8,128)}, u32[]{:S(2)}) copy-start(f32[1024,256]{1,0:T(8,128)} %param.13) | copy-start | bytes 3145732
  160.2 157.4 %all-reduce.5.cloned.1.call-start = ((), (), s32[]{:S(2)}) async-start(), calls=%async_computation.5 | async-start | bytes 4194304 | tf_op jit(solution)/shard_map/psum | solution.py:16
  230.7 148.5 %all-gather.10.cloned.1.call-start = ((), (), s32[]{:S(2)}) async-start(), calls=%async_computation.4 | async-start | bytes 9437184 | tf_op jit(solution)/shard_map/all_gather | solution.py:20
  317.6 83.4 %copy-start.1 = (bf16[256,4096]{1,0:T(8,128)(2,1)S(1)}, bf16[256,4096]{1,0:T(8,128)(2,1)}, u32[]{:S(2)}) copy-start(bf16[256,4096]{1,0:T(8,128)(2,1)} %param.7) | copy-start | bytes 6291460
Sparse Core Ops, SparseCore 0:
  15.5 113.8 all-gather.5
Sparse Core Ops, SparseCore 1:
  19.8 129.8 all-reduce.6
  160.2 50.8 all-gather.7
  230.7 86.8 all-reduce.4
  328.3 50.8 all-gather.9
where the time goes:
time: 409 us
  waiting for transfers between devices  306 us (75%)
  matrix products  40.1 us (10%)
  blocking collectives  25.9 us (6%)
  other arithmetic  19 us (5%)
  between operations  15.8 us (4%)
    all_gather x1, waiting for transfers between devices, shards(): shard_rows = lax.all_gather(local_grads, ('row', 'col'), axis=0, tiled=True)  111 us
    all_gather x2, waiting for transfers between devices, over_pieces(): blocks = lax.all_gather(value, axis)  102 us
    psum x2, waiting for transfers between devices, spread(): return lax.psum(jnp.where(mine, value, jnp.zeros_like(value)), axis)  92.9 us
    all_to_all x2, blocking collectives, from_everyone(): lax.all_to_all(jnp.broadcast_to(value[None], (peers, *value.shape)), axis...  25.9 us
    dot_general x2, matrix products, operate(): jnp.dot(gram_new, col_part, precision=lax.Precision.HIGHEST, preferred_el...  21.1 us
    dot_general x1, matrix products, shards(): lax.dot_general(left_part, right_part, (((0,), (0,)), ((), ())), preferre...  14.2 us
    reduce_sum x2, other arithmetic, over_pieces(): return blocks.sum(axis=0)  9.08 us
  transfers between devices with their start and end apart: 5, of which 5 were waited for; matrix products, arithmetic and copies ran while one was open for 4% of the time, Pallas kernels for 0%

commit v1 on v0

v1 whole, which is shorter than its diff:
```python
import functools

import jax
import jax.numpy as jnp
from jax import lax
from jax.experimental import pallas as pl
from jax.experimental.pallas import tpu as pltpu
from jax.sharding import PartitionSpec as P

MESH = pl.DeviceIdType.MESH
SEQ = 32
ITERS = 2
decay_rate = 0.5
damping = 1.0
HBM = pl.ANY


class Ring:
    def __init__(self, go, slot, lo, hi, ss, rs, base, plus, minus):
        self.go, self.slot, self.lo, self.hi = go, slot, lo, hi
        self.ss, self.rs, self.base = ss, rs, base
        self.plus, self.minus = plus, minus

    def copy(self, ref, k, dev):
        return self.go(pltpu.make_async_remote_copy(
            src_ref=ref, dst_ref=ref, send_sem=self.ss.at[self.base + k], recv_sem=self.rs.at[self.base + k],
            device_id=dev, device_id_type=MESH))

    def start(self):
        own = self.slot(0)
        self.f0 = self.copy(own, 0, self.plus)
        self.f1 = self.copy(own, 1, self.minus)

    def forward(self):
        self.f0.wait_recv()
        self.h0 = self.copy(self.lo(self.slot(3)), 2, self.plus)
        self.f1.wait_recv()
        self.h1 = self.copy(self.hi(self.slot(1)), 3, self.minus)

    def finish(self):
        self.h0.wait_recv()
        self.h1.wait_recv()


def greet(row, col):
    barrier = pltpu.get_barrier_semaphore()
    for k in range(1, 8):
        pl.semaphore_signal(barrier, inc=1, device_id=(row, lax.rem(col + k, 8)), device_id_type=MESH)
    for k in range(1, 16):
        pl.semaphore_signal(barrier, inc=1, device_id=(lax.rem(row + k, 16), col), device_id_type=MESH)
    pl.semaphore_wait(barrier, 22)


def gather_kernel(lg, left, right, loc_sem, c_send, c_recv, r_send, r_recv,
                  ya_send, ya_recv, za_send, za_recv, x_send, x_recv, p_send, p_recv):
    row = lax.axis_index("row")
    col = lax.axis_index("col")
    z, y = row // 4, row % 4
    x, core = col // 2, col % 2

    def at_col(k):
        return lax.rem(col + k, 8)

    def at_row(k):
        return lax.rem(row + k, 16)

    greet(row, col)

    def remote(src, dst, ssem, rsem, dev):
        return pltpu.make_async_remote_copy(src_ref=src, dst_ref=dst, send_sem=ssem, recv_sem=rsem,
                                            device_id=dev, device_id_type=MESH)

    sends = []

    def go(copy):
        copy.start()
        sends.append(copy)
        return copy

    own_right = pltpu.make_async_copy(lg.at[pl.ds(2 * col, 2)], right.at[:, z, y, col], loc_sem.at[0])
    own_right.start()
    own_left = pltpu.make_async_copy(lg.at[row], left.at[z, y, col], loc_sem.at[1])
    own_left.start()
    stage_c = []
    for k in (2, 6, 1, 7, 3, 5, 4):
        to = at_col(k)
        stage_c.append(go(remote(lg.at[pl.ds(2 * to, 2)], right.at[:, z, y, col],
                                 c_send.at[k], c_recv.at[k], (row, to))))
    stage_r = []
    for k in range(1, 16):
        to = at_row(k)
        stage_r.append(go(remote(lg.at[to], left.at[z, y, col], r_send.at[k], r_recv.at[k], (to, col))))

    yp, ym = z * 4 + lax.rem(y + 1, 4), z * 4 + lax.rem(y + 3, 4)
    zp, zm = lax.rem(z + 1, 4) * 4 + y, lax.rem(z + 3, 4) * 4 + y
    xp, xm = lax.rem(x + 1, 4) * 2 + core, lax.rem(x + 3, 4) * 2 + core
    partner = x * 2 + (1 - core)

    def ymod(k):
        return lax.rem(y + k, 4)

    def zmod(k):
        return lax.rem(z + k, 4)

    lo5, hi5 = (lambda r: r.at[pl.ds(0, 4)]), (lambda r: r.at[pl.ds(4, 4)])
    a0 = Ring(go, lambda k: right.at[0, z, ymod(k)], lo5, hi5, ya_send, ya_recv, 0, (yp, col), (ym, col))
    a1 = Ring(go, lambda k: right.at[1, zmod(k), y], lo5, hi5, za_send, za_recv, 0, (zp, col), (zm, col))
    b0 = [Ring(go, lambda k, j=j: right.at[0, zmod(k), ymod(j)], lo5, hi5, za_send, za_recv, 4 + 4 * j, (zp, col), (zm, col))
          for j in range(4)]
    b1 = [Ring(go, lambda k, j=j: right.at[1, zmod(j), ymod(k)], lo5, hi5, ya_send, ya_recv, 4 + 4 * j, (yp, col), (ym, col))
          for j in range(4)]
    xr = Ring(go, lambda k: left.at[:, :, lax.rem(x + k, 4) * 2 + core], lambda r: r.at[pl.ds(0, 2)], lambda r: r.at[pl.ds(2, 2)],
              x_send, x_recv, 0, (row, xp), (row, xm))

    def to_partner(k):
        c = left.at[:, :, lax.rem(x + k, 4) * 2 + core]
        return go(remote(c, c, p_send.at[k], p_recv.at[k], (row, partner)))

    own_right.wait()
    for c in stage_c:
        c.wait_recv()
    a0.start(); a1.start()
    b0[0].start(); b1[0].start()
    own_left.wait()
    for c in stage_r:
        c.wait_recv()
    xr.start()
    pp = [to_partner(0)]
    a0.forward(); a1.forward()
    for j in (3, 1):
        b0[j].start(); b1[j].start()
    xr.forward()
    pp += [to_partner(3), to_partner(1)]
    b0[0].forward(); b1[0].forward()
    a0.finish(); a1.finish()
    b0[2].start(); b1[2].start()
    xr.finish()
    pp += [to_partner(2)]
    for j in (3, 1, 2):
        b0[j].forward(); b1[j].forward()
    for j in range(4):
        b0[j].finish(); b1[j].finish()
    for c in pp:
        c.wait_recv()
    for c in sends:
        c.wait_send()


def gather(lg):
    dma = pltpu.SemaphoreType.DMA
    return pl.pallas_call(
        gather_kernel,
        out_shape=(jax.ShapeDtypeStruct((4, 4, 8, 8, 1024), jnp.bfloat16),
                   jax.ShapeDtypeStruct((2, 4, 4, 8, 8, 1024), jnp.bfloat16)),
        in_specs=[pl.BlockSpec(memory_space=pltpu.VMEM)],
        out_specs=(pl.BlockSpec(memory_space=HBM), pl.BlockSpec(memory_space=HBM)),
        scratch_shapes=[dma((2,)), dma((8,)), dma((8,)), dma((16,)), dma((16,)),
                        dma((20,)), dma((20,)), dma((20,)), dma((20,)), dma((4,)), dma((4,)), dma((4,)), dma((4,))],
        compiler_params=pltpu.CompilerParams(collective_id=0, has_side_effects=True),
        name="gather_grads",
    )(lg)


def gram_kernel(left, right, old, qt, new, gb, part, acc):
    i = pl.program_id(0)
    rows = new.shape[0]
    lt = left[...].T
    r0 = lax.axis_index("row") * 1024 + i * rows
    c0 = lax.axis_index("col") * 2048
    for h in range(2):
        sl = pl.ds(h * 1024, 1024)
        prod = jnp.dot(lt, right[h], preferred_element_type=jnp.float32)
        ri = lax.broadcasted_iota(jnp.int32, (rows, 1024), 0) + r0
        ci = lax.broadcasted_iota(jnp.int32, (rows, 1024), 1) + (c0 + h * 1024)
        g = decay_rate * old[:, sl] + ((1.0 - decay_rate) / 1024) * prod
        g = g + jnp.where(ri == ci, damping, 0.0).astype(jnp.float32)
        new[:, sl] = g
        g16 = g.astype(jnp.bfloat16)
        gb[:, sl] = g16
        add = jnp.dot(qt[...], g16, preferred_element_type=jnp.float32)

        @pl.when(i == 0)
        def _():
            acc[h] = add

        @pl.when(i > 0)
        def _():
            acc[h] += add

    @pl.when(i == pl.num_programs(0) - 1)
    def _():
        part[...] = acc[...].astype(jnp.bfloat16)


def gram(left, right, old, qt):
    rows = 256
    return pl.pallas_call(
        gram_kernel,
        grid=(1024 // rows,),
        out_shape=(jax.ShapeDtypeStruct((1024, 2048), jnp.float32),
                   jax.ShapeDtypeStruct((1024, 2048), jnp.bfloat16),
                   jax.ShapeDtypeStruct((2, 256, 1024), jnp.bfloat16)),
        in_specs=[pl.BlockSpec((1024, rows), lambda i: (0, i)),
                  pl.BlockSpec((2, 1024, 1024), lambda i: (0, 0, 0), pipeline_mode=pl.Buffered(1)),
                  pl.BlockSpec((rows, 2048), lambda i: (i, 0)),
                  pl.BlockSpec((256, rows), lambda i: (0, i))],
        out_specs=(pl.BlockSpec((rows, 2048), lambda i: (i, 0)),
                   pl.BlockSpec((rows, 2048), lambda i: (i, 0)),
                   pl.BlockSpec((2, 256, 1024), lambda i: (0, 0, 0))),
        scratch_shapes=[pltpu.VMEM((2, 256, 1024), jnp.float32)],
        name="gram_tile",
    )(left, right, old, qt)


def solve_kernel(part, gb, q, x_out, a0, a1, b0, b1, bs0, bs1, wc, wr, msg, got_r, msg2, got_c,
                 s_a, r_a, s_b, r_b, ys, yr, zs, zr, xs, xrecv, ps, pr, loc, s_r, r_r, s_c, r_c):
    row = lax.axis_index("row")
    col = lax.axis_index("col")
    z, y = row // 4, row % 4
    x, core = col // 2, col % 2
    greet(row, col)
    sends = []

    def go(copy):
        copy.start()
        sends.append(copy)
        return copy

    def remote(src, dst, ssem, rsem, dev):
        return pltpu.make_async_remote_copy(src_ref=src, dst_ref=dst, send_sem=ssem, recv_sem=rsem,
                                            device_id=dev, device_id_type=MESH)

    def ymod(k):
        return lax.rem(y + k, 4)

    def zmod(k):
        return lax.rem(z + k, 4)

    def at_y(k):
        return (z * 4 + ymod(k), col)

    def at_z(k):
        return (zmod(k) * 4 + y, col)

    c0, c1 = [], []
    for k in (1, 3, 2):
        c0.append(go(remote(part.at[0, :, ymod(k)], a0.at[k - 1], s_a.at[k], r_a.at[k], at_y(k))))
        c1.append(go(remote(part.at[1, zmod(k)], a1.at[k - 1], s_a.at[4 + k], r_a.at[4 + k], at_z(k))))
    for c in c0:
        c.wait_recv()
    f32 = jnp.float32
    t = part[0, :, y].astype(f32)
    for k in range(3):
        t += a0[k].astype(f32)
    b0[...] = t.astype(jnp.bfloat16)
    d0, d1 = [], []
    for k in (1, 3, 2):
        d0.append(go(remote(b0.at[zmod(k)], bs0.at[k - 1], s_b.at[k], r_b.at[k], at_z(k))))
    for c in c1:
        c.wait_recv()
    t = part[1, z].astype(f32)
    for k in range(3):
        t += a1[k].astype(f32)
    b1[...] = t.astype(jnp.bfloat16)
    for k in (1, 3, 2):
        d1.append(go(remote(b1.at[ymod(k)], bs1.at[k - 1], s_b.at[4 + k], r_b.at[4 + k], at_y(k))))
    lo, hi = (lambda r: r.at[:, pl.ds(0, 512)]), (lambda r: r.at[:, pl.ds(512, 512)])
    yp, ym, zp, zm = at_y(1), at_y(3), at_z(1), at_z(3)
    e0 = Ring(go, lambda k: wc.at[0, z, ymod(k)], lo, hi, ys, yr, 0, yp, ym)
    e1 = Ring(go, lambda k: wc.at[1, zmod(k), y], lo, hi, zs, zr, 0, zp, zm)
    f0 = [Ring(go, lambda k, j=j: wc.at[0, zmod(k), ymod(j)], lo, hi, zs, zr, 4 + 4 * j, zp, zm) for j in range(4)]
    f1 = [Ring(go, lambda k, j=j: wc.at[1, zmod(j), ymod(k)], lo, hi, ys, yr, 4 + 4 * j, yp, ym) for j in range(4)]
    for c in d0:
        c.wait_recv()
    t = b0[z].astype(f32)
    for k in range(3):
        t += bs0[k].astype(f32)
    wc[0, z, y] = t.astype(jnp.bfloat16)
    e0.start()
    f0[0].start()
    for c in d1:
        c.wait_recv()
    t = b1[y].astype(f32)
    for k in range(3):
        t += bs1[k].astype(f32)
    wc[1, z, y] = t.astype(jnp.bfloat16)
    e1.start()
    f1[0].start()
    e0.forward(); e1.forward()
    for j in (3, 1):
        f0[j].start(); f1[j].start()
    f0[0].forward(); f1[0].forward()
    e0.finish(); e1.finish()
    f0[2].start(); f1[2].start()
    for j in (3, 1, 2):
        f0[j].forward(); f1[j].forward()
    for j in range(4):
        f0[j].finish(); f1[j].finish()

    away = lax.rem(x - z + 4, 4)
    mine = core == y // 2
    right_dev = (row, lax.rem(x + 1, 4) * 2 + core)
    left_dev = (row, lax.rem(x + 3, 4) * 2 + core)
    partner = (row, x * 2 + 1 - core)

    def piece(ref, n):
        return ref.at[n // 2, pl.ds((n % 2) * 2, 2)]

    order = (0, 4, 1, 5, 2, 6, 3, 7)

    def along(n, dev):
        return remote(piece(wr, n), piece(wr, n), xs.at[n], xrecv.at[n], dev)

    def across(n):
        return remote(piece(wr, n), piece(wr, n), ps.at[n], pr.at[n], partner)

    @pl.when(mine)
    def _():
        @pl.when(away == 0)
        def _():
            own = pltpu.make_async_copy(wc.at[y % 2], wr, loc)
            own.start()
            own.wait()
            for n in order:
                along(n, right_dev if n < 4 else left_dev).start()
            for n in order:
                across(n).start()
            for n in order:
                along(n, right_dev).wait_send()
                across(n).wait_send()

        @pl.when(away != 0)
        def _():
            for n in order:
                along(n, right_dev).wait_recv()
                last = away == (3 if n < 4 else 1)

                @pl.when(jnp.logical_not(last))
                def _():
                    along(n, right_dev if n < 4 else left_dev).start()
                across(n).start()
            for n in order:
                last = away == (3 if n < 4 else 1)

                @pl.when(jnp.logical_not(last))
                def _():
                    along(n, right_dev).wait_send()
                across(n).wait_send()

    @pl.when(jnp.logical_not(mine))
    def _():
        for n in order:
            across(n).wait_recv()

    wrv = wr[...].reshape(256, 1024)
    v0 = jnp.dot(wrv, gb[:, :1024], preferred_element_type=f32) * wc[0].reshape(256, 1024).astype(f32)
    v1 = jnp.dot(wrv, gb[:, 1024:], preferred_element_type=f32) * wc[1].reshape(256, 1024).astype(f32)
    curve = jnp.broadcast_to(jnp.sum(v0 + v1, axis=1, keepdims=True), (256, 128)).T
    w = wrv.astype(f32).T
    qv = q[...]
    once = jnp.where(col == 0, 1.0, 0.0).astype(f32)
    msg[0:1] = jnp.sum(qv * qv, axis=0, keepdims=True) * once
    msg[1:2] = jnp.sum(qv * w, axis=0, keepdims=True) * once
    msg[2:3] = jnp.sum(w * w, axis=0, keepdims=True) * once
    msg[3:8] = curve[3:8]
    cr = [go(remote(msg, got_r.at[k], s_r.at[k], r_r.at[k], (lax.rem(row + k, 16), col))) for k in range(1, 16)]
    t = msg[...]
    for k, c in enumerate(cr):
        c.wait_recv()
        t += got_r[k + 1]
    msg2[...] = t
    cc = [go(remote(msg2, got_c.at[k], s_c.at[k], r_c.at[k], (row, lax.rem(col + k, 8)))) for k in range(1, 8)]
    for k, c in enumerate(cc):
        c.wait_recv()
        t += got_c[k + 1]
    rr, qw, ww, gg = t[0:1], t[1:2], t[2:3], t[3:4]
    s1 = rr / qw
    new = s1 * s1 * ww - rr
    beta = new / rr
    up = 1.0 + beta
    s2 = new / (up * up * qw - 2.0 * up * s1 * ww + s1 * s1 * gg)
    x_out[...] = (s1 + s2 * up) * qv - (s2 * s1) * w
    for c in sends:
        c.wait_send()


def solve(part, gb, q):
    dma = pltpu.SemaphoreType.DMA
    bf, f32 = jnp.bfloat16, jnp.float32
    vm = pltpu.VMEM
    spec = pl.BlockSpec(memory_space=pltpu.VMEM)
    return pl.pallas_call(
        solve_kernel,
        out_shape=jax.ShapeDtypeStruct((1024, 256), f32),
        in_specs=[spec, spec, spec],
        out_specs=spec,
        scratch_shapes=[vm((3, 4, 16, 1024), bf), vm((3, 4, 16, 1024), bf), vm((4, 16, 1024), bf), vm((4, 16, 1024), bf),
                        vm((3, 16, 1024), bf), vm((3, 16, 1024), bf), vm((2, 4, 4, 16, 1024), bf), vm((4, 4, 16, 1024), bf),
                        vm((8, 256), f32), vm((16, 8, 256), f32), vm((8, 256), f32), vm((8, 8, 256), f32),
                        dma((8,)), dma((8,)), dma((8,)), dma((8,)), dma((20,)), dma((20,)), dma((20,)), dma((20,)),
                        dma((8,)), dma((8,)), dma((8,)), dma((8,)), dma, dma((16,)), dma((16,)), dma((8,)), dma((8,))],
        compiler_params=pltpu.CompilerParams(collective_id=1, has_side_effects=True),
        name="solve",
    )(part, gb, q)


def shards(activations, out_grads, proj_in, proj_out, lengths, gram_old, queries):
    local_count = lengths.shape[0]
    rank = proj_in.shape[1]
    low_in = jnp.dot(activations, proj_in, preferred_element_type=jnp.float32).astype(jnp.bfloat16)
    low_out = jnp.dot(out_grads, proj_out, preferred_element_type=jnp.float32).astype(jnp.bfloat16)
    low_in = low_in.reshape(local_count, SEQ, rank)
    low_out = low_out.reshape(local_count, SEQ, rank)
    valid_mask = jnp.arange(SEQ)[None, :] < lengths[:, None]
    low_out = jnp.where(valid_mask[:, :, None], low_out, jnp.zeros((), jnp.bfloat16))
    grads = jnp.einsum("eto,eti->eoi", low_out, low_in, preferred_element_type=jnp.float32)
    lg = grads.astype(jnp.bfloat16).reshape(local_count, 16, 1024).transpose(1, 0, 2)
    left, right = gather(lg)
    left = left.reshape(1024, 1024)
    right = right.reshape(2, 1024, 1024)
    qt = queries.T.astype(jnp.bfloat16)
    gram_new, gb, part = gram(left, right, gram_old, qt)
    part = part.reshape(2, 4, 4, 16, 1024)
    return gram_new, solve(part, gb, queries)


def solution(mesh):
    in_specs = (
        P(("row", "col"), None),
        P(("row", "col"), None),
        P(),
        P(),
        P(("row", "col")),
        P("row", "col"),
        P("row", None),
    )
    out_specs = (P("row", "col"), P("row", None))
    return jax.shard_map(shards, mesh=mesh, in_specs=in_specs, out_specs=out_specs, check_vma=False)
```

time: 409 us -> 172 us (0.42)
  waiting for transfers between devices: 306 us -> 0 us
  Pallas kernels: 0 us -> 161 us
  matrix products: 40.1 us -> 2.96 us
  blocking collectives: 25.9 us -> 0 us
  other arithmetic: 19 us -> 0.88 us
  between operations: 15.8 us -> 0.72 us
  local copies, waits for them, and re-layouts: 1.62 us -> 6.62 us
    all_gather x3 -> x0, waiting for transfers between devices: 213 us -> none  [the longest x1 111 us: shards(): shard_rows = lax.all_gather(local_grads, ('row', 'col'), axis=0, tiled=True)]
    pallas_call x0 -> x3, Pallas kernels: none -> 161 us  [the longest x1 107 us: solve(): pl.pallas_call(solve_kernel, out_shape=jax.ShapeDtypeStruct((1024, 256),...]
    psum x2 -> x0, waiting for transfers between devices: 92.9 us -> none  [spread(): return lax.psum(jnp.where(mine, value, jnp.zeros_like(value)), axis)]
    dot_general x4 -> x1, matrix products: 35.7 us -> 0.35 us  [shards(): jnp.einsum('eto,eti->eoi', low_out, low_in, preferred_element_type=jnp.fl...]
    all_to_all x2 -> x0, blocking collectives: 25.9 us -> none  [from_everyone(): lax.all_to_all(jnp.broadcast_to(value[None], (peers, *value.shape)), axis...]
    reduce_sum x6 -> x0, other arithmetic: 10.8 us -> none  [the longest x2 9.08 us: over_pieces(): return blocks.sum(axis=0)]
    select_n x3 -> x0, other arithmetic: 4.9 us -> none  [spread(): return lax.psum(jnp.where(mine, value, jnp.zeros_like(value)), axis)]
  transfers between devices with their start and end apart: 5 -> 0, of which waited for: 5 -> 0; matrix products, arithmetic and copies ran while one was open for 4% -> 0% of each run, Pallas kernels for 0% -> 0%
where the time goes in v1:
time: 172 us
  Pallas kernels  161 us (94%)
  local copies, waits for them, and re-layouts  6.62 us (4%)
  matrix products  2.96 us (2%)
    pallas_call x1, Pallas kernels, solve(): pl.pallas_call(solve_kernel, out_shape=jax.ShapeDtypeStruct((1024, 256),...  107 us
    pallas_call x1, Pallas kernels, gather(): pl.pallas_call(gather_kernel, out_shape=(jax.ShapeDtypeStruct((4, 4, 8, 8...  38.6 us
    pallas_call x1, Pallas kernels, gram(): pl.pallas_call(gram_kernel, grid=(1024 // rows,), out_shape=(jax.ShapeDty...  15.3 us
    unnamed x10, local copies, waits for them, and re-layouts  4.01 us

profile of v1, /device:TPU:1, one launch (start us, length us, event | category | flops | bytes accessed | tf_op | source)
XLA Modules:
  0.0 172.0 jit_solution(15943762612412311416)
XLA Ops:
  0.6 0.0 copy-start
  0.6 0.0 copy-start.3
  0.7 0.0 copy-start.2
  0.7 0.9 iota_compare_fusion
  1.5 0.7 copy-done
  2.2 1.9 %convolution_convert_fusion.1 = bf16[256,128]{1,0:T(8,128)(2,1)S(1)} fusion(bf16[256,4096]{1,0:T(8,128)(2,1)S(1)} %copy-done, bf16[4096,128]{1,0:T(8,128)(2,1)} %param.9), kind=kOutput, calls=%fused_computation.1 | convolution fusion | flops 268468224 | bytes 3211264 | tf_op jit(solution)/shard_map/dot_general | solution.py:410
  4.2 0.0 copy-done.3
  4.2 0.0 copy-done.2
  4.2 0.0 copy-start.1
  4.2 0.7 convolution_convert_fusion.2
  4.9 0.3 convolution_convert_fusion
  5.3 0.8 reshape.45
  6.1 1.8 %copy.13 = bf16[8,16,1024]{2,0,1:T(8,128)(2,1)} copy(bf16[8,16,1024]{2,1,0:T(8,128)(2,1)} %reshape.45) | data formatting | bytes 524288 | tf_op jit(solution)/shard_map/reshape | solution.py:417
  7.9 0.0 copy-done.1
  7.9 1.0 copy.11
  8.9 38.6 %gather_grads.1 = (bf16[4,4,8,8,1024]{4,3,2,1,0:T(8,128)(2,1)}, bf16[2,4,4,8,8,1024]{5,4,3,2,1,0:T(8,128)(2,1)}) custom-call(bf16[16,8,1024]{2,1,0:T(8,128)(2,1)} %bitcast.20), custom_call_target="tpu_custom_call" | custom-call | tf_op jit(solution)/shard_map/gather_grads/pallas_call | solution.py:151
  47.5 15.3 %gram_tile.1 = (f32[1024,2048]{1,0:T(8,128)}, bf16[1024,2048]{1,0:T(8,128)(2,1)}, bf16[2,256,1024]{2,1,0:T(8,128)(2,1)}) custom-call(bf16[1024,1024]{1,0:T(8,128)(2,1)} %bitcast.17, bf16[2,1024,1024]{2,1,0:T(8,128)(2,1)} %bitcast.16, f32[1024,2048]{1,0:T(8,128)} %old.1, bf16[256,1024]{1,0:T(8,128)(2,1)} %bitcast.18), custom_call_target="tpu_custom_call" | custom-call | tf_op jit(solution)/shard_map/gram_tile/pallas_call | solution.py:197
  62.8 106.9 %solve.1 = f32[1024,256]{1,0:T(8,128)} custom-call(bf16[2,4,4,16,1024]{4,3,2,1,0:T(8,128)(2,1)} %bitcast.19, bf16[1024,2048]{1,0:T(8,128)(2,1)} %get-tuple-element.11.gb, f32[1024,256]{1,0:T(8,128)} %q.1), custom_call_target="tpu_custom_call" | custom-call | tf_op jit(solution)/shard_map/solve/pallas_call | solution.py:392
  169.7 2.3 %copy.15 = f32[1024,256]{1,0:T(8,128)} copy(f32[1024,256]{1,0:T(8,128)} %solve.1) | data formatting | bytes 2097152
Async XLA Ops:
  0.6 1.6 copy-start
  0.6 3.5 %copy-start.3 = (bf16[4096,128]{1,0:T(8,128)(2,1)S(1)}, bf16[4096,128]{1,0:T(8,128)(2,1)}, u32[]{:S(2)}) copy-start(bf16[4096,128]{1,0:T(8,128)(2,1)} %param.10) | copy-start | bytes 3145732
  0.7 3.5 %copy-start.2 = (bf16[256,4096]{1,0:T(8,128)(2,1)S(1)}, bf16[256,4096]{1,0:T(8,128)(2,1)}, u32[]{:S(2)}) copy-start(bf16[256,4096]{1,0:T(8,128)(2,1)} %param.8) | copy-start | bytes 6291460
  4.2 3.7 %copy-start.1 = (f32[1024,256]{1,0:T(8,128)S(1)}, f32[1024,256]{1,0:T(8,128)}, u32[]{:S(2)}) copy-start(f32[1024,256]{1,0:T(8,128)} %q.1) | copy-start | bytes 3145732

commit v2 on v1

v2 whole, which is shorter than its diff:
```python
import functools

import jax
import jax.numpy as jnp
from jax import lax
from jax.experimental import pallas as pl
from jax.experimental.pallas import tpu as pltpu
from jax.sharding import PartitionSpec as P

MESH = pl.DeviceIdType.MESH
SEQ = 32
ITERS = 2
decay_rate = 0.5
damping = 1.0
HBM = pl.ANY


class Ring:
    def __init__(self, go, slot, lo, hi, ss, rs, base, plus, minus):
        self.go, self.slot, self.lo, self.hi = go, slot, lo, hi
        self.ss, self.rs, self.base = ss, rs, base
        self.plus, self.minus = plus, minus

    def copy(self, ref, k, dev):
        return self.go(pltpu.make_async_remote_copy(
            src_ref=ref, dst_ref=ref, send_sem=self.ss.at[self.base + k], recv_sem=self.rs.at[self.base + k],
            device_id=dev, device_id_type=MESH))

    def start(self):
        own = self.slot(0)
        self.f0 = self.copy(own, 0, self.plus)
        self.f1 = self.copy(own, 1, self.minus)

    def forward(self):
        self.f0.wait_recv()
        self.h0 = self.copy(self.lo(self.slot(3)), 2, self.plus)
        self.f1.wait_recv()
        self.h1 = self.copy(self.hi(self.slot(1)), 3, self.minus)

    def finish(self):
        self.h0.wait_recv()
        self.h1.wait_recv()


def greet(row, col):
    barrier = pltpu.get_barrier_semaphore()
    for k in range(1, 8):
        pl.semaphore_signal(barrier, inc=1, device_id=(row, lax.rem(col + k, 8)), device_id_type=MESH)
    for k in range(1, 16):
        pl.semaphore_signal(barrier, inc=1, device_id=(lax.rem(row + k, 16), col), device_id_type=MESH)
    pl.semaphore_wait(barrier, 22)


def gather_kernel(lg, q, left_t, right, qt, left, loc_sem, c_send, c_recv, r_send, r_recv,
                  ya_send, ya_recv, za_send, za_recv, x_send, x_recv, p_send, p_recv):
    row = lax.axis_index("row")
    col = lax.axis_index("col")
    z, y = row // 4, row % 4
    x, core = col // 2, col % 2

    def at_col(k):
        return lax.rem(col + k, 8)

    def at_row(k):
        return lax.rem(row + k, 16)

    greet(row, col)

    def remote(src, dst, ssem, rsem, dev):
        return pltpu.make_async_remote_copy(src_ref=src, dst_ref=dst, send_sem=ssem, recv_sem=rsem,
                                            device_id=dev, device_id_type=MESH)

    sends = []

    def go(copy):
        copy.start()
        sends.append(copy)
        return copy

    own_right = pltpu.make_async_copy(lg.at[pl.ds(2 * col, 2)], right.at[:, z, y, col], loc_sem.at[0])
    own_right.start()
    own_left = pltpu.make_async_copy(lg.at[row], left.at[z, y, col], loc_sem.at[1])
    own_left.start()
    stage_c = []
    for k in (2, 6, 1, 7, 3, 5, 4):
        to = at_col(k)
        stage_c.append(go(remote(lg.at[pl.ds(2 * to, 2)], right.at[:, z, y, col],
                                 c_send.at[k], c_recv.at[k], (row, to))))
    stage_r = []
    for k in range(1, 16):
        to = at_row(k)
        stage_r.append(go(remote(lg.at[to], left.at[z, y, col], r_send.at[k], r_recv.at[k], (to, col))))

    yp, ym = z * 4 + lax.rem(y + 1, 4), z * 4 + lax.rem(y + 3, 4)
    zp, zm = lax.rem(z + 1, 4) * 4 + y, lax.rem(z + 3, 4) * 4 + y
    xp, xm = lax.rem(x + 1, 4) * 2 + core, lax.rem(x + 3, 4) * 2 + core
    partner = x * 2 + (1 - core)

    def ymod(k):
        return lax.rem(y + k, 4)

    def zmod(k):
        return lax.rem(z + k, 4)

    lo5, hi5 = (lambda r: r.at[pl.ds(0, 4)]), (lambda r: r.at[pl.ds(4, 4)])
    a0 = Ring(go, lambda k: right.at[0, z, ymod(k)], lo5, hi5, ya_send, ya_recv, 0, (yp, col), (ym, col))
    a1 = Ring(go, lambda k: right.at[1, zmod(k), y], lo5, hi5, za_send, za_recv, 0, (zp, col), (zm, col))
    b0 = [Ring(go, lambda k, j=j: right.at[0, zmod(k), ymod(j)], lo5, hi5, za_send, za_recv, 4 + 4 * j, (zp, col), (zm, col))
          for j in range(4)]
    b1 = [Ring(go, lambda k, j=j: right.at[1, zmod(j), ymod(k)], lo5, hi5, ya_send, ya_recv, 4 + 4 * j, (yp, col), (ym, col))
          for j in range(4)]
    xr = Ring(go, lambda k: left.at[:, :, lax.rem(x + k, 4) * 2 + core], lambda r: r.at[pl.ds(0, 2)], lambda r: r.at[pl.ds(2, 2)],
              x_send, x_recv, 0, (row, xp), (row, xm))

    def to_partner(k):
        c = left.at[:, :, lax.rem(x + k, 4) * 2 + core]
        return go(remote(c, c, p_send.at[k], p_recv.at[k], (row, partner)))

    own_right.wait()
    own_left.wait()
    for c in stage_c:
        c.wait_recv()
    a0.start(); a1.start()
    b0[0].start(); b1[0].start()
    for c in stage_r:
        c.wait_recv()
    xr.start()
    pp = [to_partner(0)]
    a0.forward(); a1.forward()
    for j in (3, 1):
        b0[j].start(); b1[j].start()
    xr.forward()
    pp += [to_partner(3), to_partner(1)]
    b0[0].forward(); b1[0].forward()
    a0.finish(); a1.finish()
    b0[2].start(); b1[2].start()
    xr.finish()
    pp += [to_partner(2)]
    for j in (3, 1, 2):
        b0[j].forward(); b1[j].forward()
    for c in pp:
        c.wait_recv()
    for n in range(8):
        pair = left[n // 2, pl.ds(2 * (n % 2), 2)].astype(jnp.float32).reshape(128, 1024)
        left_t[:, pl.ds(n * 128, 128)] = pair.T.astype(jnp.bfloat16)
    qt[...] = q[...].T.astype(jnp.bfloat16)
    for j in range(4):
        b0[j].finish(); b1[j].finish()
    for c in sends:
        c.wait_send()


def gather(lg, q):
    dma = pltpu.SemaphoreType.DMA
    return pl.pallas_call(
        gather_kernel,
        out_shape=(jax.ShapeDtypeStruct((1024, 1024), jnp.bfloat16),
                   jax.ShapeDtypeStruct((2, 4, 4, 8, 8, 1024), jnp.bfloat16),
                   jax.ShapeDtypeStruct((256, 1024), jnp.bfloat16)),
        in_specs=[pl.BlockSpec(memory_space=pltpu.VMEM)] * 2,
        out_specs=(pl.BlockSpec(memory_space=pltpu.VMEM), pl.BlockSpec(memory_space=HBM),
                   pl.BlockSpec(memory_space=pltpu.VMEM)),
        scratch_shapes=[pltpu.VMEM((4, 4, 8, 8, 1024), jnp.bfloat16), dma((2,)), dma((8,)), dma((8,)), dma((16,)), dma((16,)),
                        dma((20,)), dma((20,)), dma((20,)), dma((20,)), dma((4,)), dma((4,)), dma((4,)), dma((4,))],
        compiler_params=pltpu.CompilerParams(collective_id=0, has_side_effects=True),
        name="gather_grads",
    )(lg, q)


def gram_kernel(left_t, right, old, qt, new, gb, part):
    j = pl.program_id(0)
    cols = new.shape[1]
    f32 = jnp.float32
    prod = jnp.dot(left_t[...], right[0], preferred_element_type=f32)
    off = lax.axis_index("col") * 2048 + j * cols - lax.axis_index("row") * 1024
    ri = lax.broadcasted_iota(jnp.int32, prod.shape, 0)
    ci = lax.broadcasted_iota(jnp.int32, prod.shape, 1) + off
    g = decay_rate * old[...] + ((1.0 - decay_rate) / 1024) * prod
    g = g + jnp.where(ri == ci, damping, 0.0).astype(f32)
    new[...] = g
    g16 = g.astype(jnp.bfloat16)
    gb[...] = g16
    part[0] = jnp.dot(qt[...], g16, preferred_element_type=f32).astype(jnp.bfloat16)


def gram(left_t, right, old, qt):
    cols = 256
    n = 1024 // cols
    return pl.pallas_call(
        gram_kernel,
        grid=(2048 // cols,),
        out_shape=(jax.ShapeDtypeStruct((1024, 2048), jnp.float32),
                   jax.ShapeDtypeStruct((1024, 2048), jnp.bfloat16),
                   jax.ShapeDtypeStruct((2, 256, 1024), jnp.bfloat16)),
        in_specs=[pl.BlockSpec((1024, 1024), lambda j: (0, 0), pipeline_mode=pl.Buffered(1)),
                  pl.BlockSpec((1, 1024, cols), lambda j: (j // n, 0, j % n)),
                  pl.BlockSpec((1024, cols), lambda j: (0, j)),
                  pl.BlockSpec((256, 1024), lambda j: (0, 0), pipeline_mode=pl.Buffered(1))],
        out_specs=(pl.BlockSpec((1024, cols), lambda j: (0, j)),
                   pl.BlockSpec((1024, cols), lambda j: (0, j)),
                   pl.BlockSpec((1, 256, cols), lambda j: (j // n, 0, j % n))),
        name="gram_tile",
    )(left_t, right, old, qt)


def solve_kernel(part, gb, q, x_out, a_far, a_got, a_sum, b_sum, b_got, wc, wr, msg, got_r, msg2, got_c,
                 s_a, r_a, s_b, r_b, ys, yr, zs, zr, xs, xrecv, ps, pr, s_r, r_r, s_c, r_c):
    row = lax.axis_index("row")
    col = lax.axis_index("col")
    z, y = row // 4, row % 4
    x, core = col // 2, col % 2
    greet(row, col)
    sends = []

    def go(copy):
        copy.start()
        sends.append(copy)
        return copy

    def remote(src, dst, ssem, rsem, dev):
        return pltpu.make_async_remote_copy(src_ref=src, dst_ref=dst, send_sem=ssem, recv_sem=rsem,
                                            device_id=dev, device_id_type=MESH)

    def ymod(k):
        return lax.rem(y + k, 4)

    def zmod(k):
        return lax.rem(z + k, 4)

    def at_y(k):
        return (z * 4 + ymod(k), col)

    def at_z(k):
        return (zmod(k) * 4 + y, col)

    f32, bf = jnp.float32, jnp.bfloat16
    yp, ym, zp, zm = at_y(1), at_y(3), at_z(1), at_z(3)
    lo, hi = pl.ds(0, 512), pl.ds(512, 512)

    def chunk(h, k):
        return part.at[0, :, ymod(k)] if h == 0 else part.at[1, zmod(k)]

    near = ((yp, ym), (zp, zm))
    far, plain = [], []
    for h in range(2):
        plus, minus = near[h]
        far.append((go(remote(chunk(h, 2).at[:, :, lo], a_far.at[h, 0], s_a.at[h, 0], r_a.at[h, 0], plus)),
                    go(remote(chunk(h, 2).at[:, :, hi], a_far.at[h, 1], s_a.at[h, 1], r_a.at[h, 1], minus))))
    for h in range(2):
        plus, minus = near[h]
        plain.append((go(remote(chunk(h, 1).at[:, :, hi], a_got.at[h, 0, 1], s_a.at[h, 2], r_a.at[h, 2], plus)),
                      go(remote(chunk(h, 3).at[:, :, lo], a_got.at[h, 1, 0], s_a.at[h, 3], r_a.at[h, 3], minus))))
    joined = []
    for h in range(2):
        plus, minus = near[h]
        far[h][0].wait_recv()
        a_sum[h, 0] = (chunk(h, 1)[:, :, lo].astype(f32) + a_far[h, 0].astype(f32)).astype(bf)
        up = go(remote(a_sum.at[h, 0], a_got.at[h, 0, 0], s_a.at[h, 4], r_a.at[h, 4], plus))
        far[h][1].wait_recv()
        a_sum[h, 1] = (chunk(h, 3)[:, :, hi].astype(f32) + a_far[h, 1].astype(f32)).astype(bf)
        joined.append((up, go(remote(a_sum.at[h, 1], a_got.at[h, 1, 1], s_a.at[h, 5], r_a.at[h, 5], minus))))
    second = []
    for h in range(2):
        for c in plain[h] + joined[h]:
            c.wait_recv()
        for n, lanes in enumerate((lo, hi)):
            t = chunk(h, 0)[:, :, lanes].astype(f32) + a_got[h, 0, n].astype(f32) + a_got[h, 1, n].astype(f32)
            b_sum[h, :, :, lanes] = t.astype(bf)
        second.append([])
        for k in (1, 3, 2):
            to, dev = (zmod(k), at_z(k)) if h == 0 else (ymod(k), at_y(k))
            second[h].append(go(remote(b_sum.at[h, to], b_got.at[h, k - 1], s_b.at[h, k], r_b.at[h, k], dev)))

    lol, hil = (lambda r: r.at[:, lo]), (lambda r: r.at[:, hi])
    e0 = Ring(go, lambda k: wc.at[0, z, ymod(k)], lol, hil, ys, yr, 0, yp, ym)
    e1 = Ring(go, lambda k: wc.at[1, zmod(k), y], lol, hil, zs, zr, 0, zp, zm)
    f0 = [Ring(go, lambda k, j=j: wc.at[0, zmod(k), ymod(j)], lol, hil, zs, zr, 4 + 4 * j, zp, zm) for j in range(4)]
    f1 = [Ring(go, lambda k, j=j: wc.at[1, zmod(j), ymod(k)], lol, hil, ys, yr, 4 + 4 * j, yp, ym) for j in range(4)]
    half = y % 2
    mine = core == y // 2
    root = jnp.logical_and(mine, x == z)
    partner = (row, x * 2 + 1 - core)
    pieces = []

    def group(late, early):
        dz = jnp.where(half == 0, late, early)
        dy = jnp.where(half == 0, early, late)
        return zmod(dz), ymod(dy)

    def along(n, k):
        gz, gy = pieces[n]
        return remote(wc.at[half, gz, gy], wr.at[gz, gy], xs.at[n, k], xrecv.at[n], (row, lax.rem(x + k, 4) * 2 + core))

    def across(n, src):
        gz, gy = pieces[n]
        return remote(src.at[gz, gy], wr.at[gz, gy], ps.at[n], pr.at[n], partner)

    def publish(*which):
        first = len(pieces)
        pieces.extend(group(*w) for w in which)

        @pl.when(root)
        def _():
            for n in range(first, len(pieces)):
                for k in (1, 3, 2):
                    along(n, k).start()
                across(n, wc.at[half]).start()

    for h in range(2):
        for c in second[h]:
            c.wait_recv()
        t = b_sum[h, z if h == 0 else y].astype(f32)
        for k in range(3):
            t += b_got[h, k].astype(f32)
        wc[h, z, y] = t.astype(bf)
        (e0, e1)[h].start()
        (f0, f1)[h][0].start()
    publish((0, 0))
    e0.forward(); e1.forward()
    for j in (3, 1):
        f0[j].start(); f1[j].start()
    publish((0, 3), (0, 1))
    f0[0].forward(); f1[0].forward()
    e0.finish(); e1.finish()
    f0[2].start(); f1[2].start()
    publish((3, 0), (1, 0), (0, 2))
    for j in (3, 1, 2):
        f0[j].forward(); f1[j].forward()
        publish((3, j), (1, j))
    for j in (0, 3, 1, 2):
        f0[j].finish(); f1[j].finish()
        publish((2, j))

    @pl.when(root)
    def _():
        wr[...] = wc[half]
        for n in range(16):
            for k in (1, 3, 2):
                along(n, k).wait_send()
            across(n, wc.at[half]).wait_send()

    @pl.when(jnp.logical_and(mine, x != z))
    def _():
        for n in range(16):
            along(n, 1).wait_recv()
            across(n, wr).start()
        for n in range(16):
            across(n, wr).wait_send()

    @pl.when(jnp.logical_not(mine))
    def _():
        for n in range(16):
            across(n, wr).wait_recv()

    wrv = wr[...].reshape(256, 1024)
    v0 = jnp.dot(wrv, gb[:, :1024], preferred_element_type=f32) * wc[0].reshape(256, 1024).astype(f32)
    v1 = jnp.dot(wrv, gb[:, 1024:], preferred_element_type=f32) * wc[1].reshape(256, 1024).astype(f32)
    curve = jnp.broadcast_to(jnp.sum(v0 + v1, axis=1, keepdims=True), (256, 128)).T
    w = wrv.astype(f32).T
    qv = q[...]
    once = jnp.where(col == 0, 1.0, 0.0).astype(f32)
    msg[0:1] = jnp.sum(qv * qv, axis=0, keepdims=True) * once
    msg[1:2] = jnp.sum(qv * w, axis=0, keepdims=True) * once
    msg[2:3] = jnp.sum(w * w, axis=0, keepdims=True) * once
    msg[3:4] = curve[3:4]
    cr = [go(remote(msg, got_r.at[k], s_r.at[k], r_r.at[k], (lax.rem(row + k, 16), col))) for k in range(1, 16)]
    t = msg[...]
    for k, c in enumerate(cr):
        c.wait_recv()
        t += got_r[k + 1]
    msg2[...] = t
    cc = [go(remote(msg2, got_c.at[k], s_c.at[k], r_c.at[k], (row, lax.rem(col + k, 8)))) for k in range(1, 8)]
    for k, c in enumerate(cc):
        c.wait_recv()
        t += got_c[k + 1]
    rr, qw, ww, gg = t[0:1], t[1:2], t[2:3], t[3:4]
    s1 = rr / qw
    new = s1 * s1 * ww - rr
    beta = new / rr
    up = 1.0 + beta
    s2 = new / (up * up * qw - 2.0 * up * s1 * ww + s1 * s1 * gg)
    x_out[...] = (s1 + s2 * up) * qv - (s2 * s1) * w
    for c in sends:
        c.wait_send()


def solve(part, gb, q):
    dma = pltpu.SemaphoreType.DMA
    bf, f32 = jnp.bfloat16, jnp.float32
    vm = pltpu.VMEM
    spec = pl.BlockSpec(memory_space=pltpu.VMEM)
    return pl.pallas_call(
        solve_kernel,
        out_shape=jax.ShapeDtypeStruct((1024, 256), f32),
        in_specs=[spec, spec, spec],
        out_specs=spec,
        scratch_shapes=[vm((2, 2, 4, 16, 512), bf), vm((2, 2, 2, 4, 16, 512), bf), vm((2, 2, 4, 16, 512), bf), vm((2, 4, 16, 1024), bf),
                        vm((2, 3, 16, 1024), bf), vm((2, 4, 4, 16, 1024), bf), vm((4, 4, 16, 1024), bf),
                        vm((4, 256), f32), vm((16, 4, 256), f32), vm((4, 256), f32), vm((8, 4, 256), f32),
                        dma((2, 6)), dma((2, 6)), dma((2, 4)), dma((2, 4)), dma((20,)), dma((20,)), dma((20,)), dma((20,)),
                        dma((16, 4)), dma((16,)), dma((16,)), dma((16,)), dma((16,)), dma((16,)), dma((8,)), dma((8,))],
        compiler_params=pltpu.CompilerParams(collective_id=1, has_side_effects=True),
        name="solve",
    )(part, gb, q)


def shards(activations, out_grads, proj_in, proj_out, lengths, gram_old, queries):
    local_count = lengths.shape[0]
    rank = proj_in.shape[1]
    low_in = jnp.dot(activations, proj_in, preferred_element_type=jnp.float32).astype(jnp.bfloat16)
    low_out = jnp.dot(out_grads, proj_out, preferred_element_type=jnp.float32).astype(jnp.bfloat16)
    low_in = low_in.reshape(local_count, SEQ, rank)
    low_out = low_out.reshape(local_count, SEQ, rank)
    valid_mask = jnp.arange(SEQ)[None, :] < lengths[:, None]
    low_out = jnp.where(valid_mask[:, :, None], low_out, jnp.zeros((), jnp.bfloat16))
    grads = jnp.einsum("eto,eti->eoi", low_out, low_in, preferred_element_type=jnp.float32)
    lg = grads.astype(jnp.bfloat16).reshape(local_count, 16, 1024).transpose(1, 0, 2)
    left, right, qt = gather(lg, queries)
    right = right.reshape(2, 1024, 1024)
    gram_new, gb, part = gram(left, right, gram_old, qt)
    part = part.reshape(2, 4, 4, 16, 1024)
    return gram_new, solve(part, gb, queries)


def solution(mesh):
    in_specs = (
        P(("row", "col"), None),
        P(("row", "col"), None),
        P(),
        P(),
        P(("row", "col")),
        P("row", "col"),
        P("row", None),
    )
    out_specs = (P("row", "col"), P("row", None))
    return jax.shard_map(shards, mesh=mesh, in_specs=in_specs, out_specs=out_specs, check_vma=False)
```

time: 172 us -> 116 us (0.67)
  Pallas kernels: 161 us -> 107 us
  local copies, waits for them, and re-layouts: 6.62 us -> 3.95 us
    pallas_call x1, Pallas kernels: 107 us -> 52.6 us  [solve(): pl.pallas_call(solve_kernel, out_shape=jax.ShapeDtypeStruct((1024, 256),...]
    unnamed x10 -> x7, local copies, waits for them, and re-layouts: 4.01 us -> 2.98 us
where the time goes in v2:
time: 116 us
  Pallas kernels  107 us (92%)
  local copies, waits for them, and re-layouts  3.95 us (3%)
  matrix products  2.96 us (3%)
    pallas_call x1, Pallas kernels, solve(): pl.pallas_call(solve_kernel, out_shape=jax.ShapeDtypeStruct((1024, 256),...  52.6 us
    pallas_call x1, Pallas kernels, gather(): pl.pallas_call(gather_kernel, out_shape=(jax.ShapeDtypeStruct((1024, 1024...  40.3 us
    pallas_call x1, Pallas kernels, gram(): pl.pallas_call(gram_kernel, grid=(2048 // cols,), out_shape=(jax.ShapeDty...  14.5 us
    unnamed x7, local copies, waits for them, and re-layouts  2.98 us

profile of v2, /device:TPU:1, one launch (start us, length us, event | category | flops | bytes accessed | tf_op | source)
XLA Modules:
  0.0 115.9 jit_solution(5184196197817328742)
XLA Ops:
  0.6 0.0 copy-start
  0.6 0.0 copy-start.2
  0.7 0.0 copy-start.1
  0.7 0.9 iota_compare_fusion
  1.5 0.7 copy-done
  2.2 1.9 %convolution_convert_fusion.1 = bf16[256,128]{1,0:T(8,128)(2,1)S(1)} fusion(bf16[256,4096]{1,0:T(8,128)(2,1)S(1)} %copy-done, bf16[4096,128]{1,0:T(8,128)(2,1)} %param.9), kind=kOutput, calls=%fused_computation.1 | convolution fusion | flops 268468224 | bytes 3211264 | tf_op jit(solution)/shard_map/dot_general | solution.py:410
  4.2 0.0 copy-done.2
  4.2 0.0 copy-done.1
  4.2 0.7 convolution_convert_fusion.2
  4.9 0.3 convolution_convert_fusion
  5.2 0.1 reshape.42
  5.4 0.9 copy.11
  6.2 40.3 %gather_grads.1 = (bf16[1024,1024]{1,0:T(8,128)(2,1)}, bf16[2,4,4,8,8,1024]{5,4,3,2,1,0:T(8,128)(2,1)}, bf16[256,1024]{1,0:T(8,128)(2,1)}) custom-call(bf16[16,8,1024]{2,1,0:T(8,128)(2,1)} %bitcast.14, f32[1024,256]{1,0:T(8,128)} %q.3), custom_call_target="tpu_custom_call" | custom-call | tf_op jit(solution)/shard_map/gather_grads/pallas_call | solution.py:155
  46.6 14.5 %gram_tile.1 = (f32[1024,2048]{1,0:T(8,128)}, bf16[1024,2048]{1,0:T(8,128)(2,1)}, bf16[2,256,1024]{2,1,0:T(8,128)(2,1)}) custom-call(bf16[1024,1024]{1,0:T(8,128)(2,1)} %get-tuple-element.8.left_t, bf16[2,1024,1024]{2,1,0:T(8,128)(2,1)} %bitcast.12, f32[1024,2048]{1,0:T(8,128)} %old.1, bf16[256,1024]{1,0:T(8,128)(2,1)} %get-tuple-element.10.qt), custom_call_target="tpu_custom_call" | custom-call | tf_op jit(solution)/shard_map/gram_tile/pallas_call | solution.py:189
  61.0 52.6 %solve.1 = f32[1024,256]{1,0:T(8,128)} custom-call(bf16[2,4,4,16,1024]{4,3,2,1,0:T(8,128)(2,1)} %bitcast.13, bf16[1024,2048]{1,0:T(8,128)(2,1)} %get-tuple-element.13.gb, f32[1024,256]{1,0:T(8,128)} %q.3), custom_call_target="tpu_custom_call" | custom-call | tf_op jit(solution)/shard_map/solve/pallas_call | solution.py:392
  113.6 2.3 %copy.13 = f32[1024,256]{1,0:T(8,128)} copy(f32[1024,256]{1,0:T(8,128)} %solve.1) | data formatting | bytes 2097152
Async XLA Ops:
  0.6 1.6 %copy-start = (bf16[256,4096]{1,0:T(8,128)(2,1)S(1)}, bf16[256,4096]{1,0:T(8,128)(2,1)}, u32[]{:S(2)}) copy-start(bf16[256,4096]{1,0:T(8,128)(2,1)} %param.7) | copy-start | bytes 6291460
  0.6 3.5 %copy-start.2 = (bf16[4096,128]{1,0:T(8,128)(2,1)S(1)}, bf16[4096,128]{1,0:T(8,128)(2,1)}, u32[]{:S(2)}) copy-start(bf16[4096,128]{1,0:T(8,128)(2,1)} %param.10) | copy-start | bytes 3145732
  0.7 3.5 %copy-start.1 = (bf16[256,4096]{1,0:T(8,128)(2,1)S(1)}, bf16[256,4096]{1,0:T(8,128)(2,1)}, u32[]{:S(2)}) copy-start(bf16[256,4096]{1,0:T(8,128)(2,1)} %param.8) | copy-start | bytes 6291460

commit v3 on v2

v3 whole, which is shorter than its diff:
```python
import functools

import jax
import jax.numpy as jnp
from jax import lax
from jax.experimental import pallas as pl
from jax.experimental.pallas import tpu as pltpu
from jax.sharding import PartitionSpec as P

MESH = pl.DeviceIdType.MESH
SEQ = 32
ITERS = 2
decay_rate = 0.5
damping = 1.0
HBM = pl.ANY


class Ring:
    def __init__(self, go, slot, lo, hi, ss, rs, base, plus, minus):
        self.go, self.slot, self.lo, self.hi = go, slot, lo, hi
        self.ss, self.rs, self.base = ss, rs, base
        self.plus, self.minus = plus, minus

    def copy(self, ref, k, dev):
        return self.go(pltpu.make_async_remote_copy(
            src_ref=ref, dst_ref=ref, send_sem=self.ss.at[self.base + k], recv_sem=self.rs.at[self.base + k],
            device_id=dev, device_id_type=MESH))

    def start(self):
        own = self.slot(0)
        self.f0 = self.copy(own, 0, self.plus)
        self.f1 = self.copy(own, 1, self.minus)

    def forward(self):
        self.f0.wait_recv()
        self.h0 = self.copy(self.lo(self.slot(3)), 2, self.plus)
        self.f1.wait_recv()
        self.h1 = self.copy(self.hi(self.slot(1)), 3, self.minus)

    def finish(self):
        self.h0.wait_recv()
        self.h1.wait_recv()


def greet(row, col):
    barrier = pltpu.get_barrier_semaphore()
    for k in range(1, 8):
        pl.semaphore_signal(barrier, inc=1, device_id=(row, lax.rem(col + k, 8)), device_id_type=MESH)
    for k in range(1, 16):
        pl.semaphore_signal(barrier, inc=1, device_id=(lax.rem(row + k, 16), col), device_id_type=MESH)
    return barrier


def kernel(act, og, p_in, p_out, lens, old_hbm, q_hbm, new, x_out,
           act_v, og_v, pin_v, pout_v, old, q, lg, left, right, qt, acc, gb, part,
           a_far, a_got, a_sum, b_sum, b_got, wc, wr, msg, got_r, msg2, got_c,
           in_sem, out_sem, loc_sem, c_send, c_recv, r_send, r_recv, ya_send, ya_recv, za_send, za_recv,
           x_send, x_recv, p_send, p_recv,
           s_a, r_a, s_b, r_b, ys, yr, zs, zr, xs, xrecv, ps, pr, s_r, r_r, s_c, r_c):
    f32, bf = jnp.float32, jnp.bfloat16
    row = lax.axis_index("row")
    col = lax.axis_index("col")
    z, y = row // 4, row % 4
    x, core = col // 2, col % 2
    barrier = greet(row, col)
    loads = [pltpu.make_async_copy(a, b, in_sem.at[n]) for n, (a, b) in enumerate(
        ((p_out, pout_v), (og, og_v), (p_in, pin_v), (act, act_v), (q_hbm, q), (old_hbm, old)))]
    for c in loads[:4]:
        c.start()
    sends = []

    def go(copy):
        copy.start()
        sends.append(copy)
        return copy

    def remote(src, dst, ssem, rsem, dev):
        return pltpu.make_async_remote_copy(src_ref=src, dst_ref=dst, send_sem=ssem, recv_sem=rsem,
                                            device_id=dev, device_id_type=MESH)

    def ymod(k):
        return lax.rem(y + k, 4)

    def zmod(k):
        return lax.rem(z + k, 4)

    def at_y(k):
        return (z * 4 + ymod(k), col)

    def at_z(k):
        return (zmod(k) * 4 + y, col)

    loads[0].wait()
    loads[1].wait()
    low_out = jnp.dot(og_v[...], pout_v[...], preferred_element_type=f32).astype(bf).astype(f32).T
    ex = lax.broadcasted_iota(jnp.int32, (8, 256), 0)
    slot = lax.broadcasted_iota(jnp.int32, (8, 256), 1) - SEQ * ex
    count = jnp.zeros((8, 256), jnp.int32)
    for e in range(8):
        count = jnp.where(ex == e, lens[e], count)
    valid = jnp.logical_and(slot >= 0, slot < jnp.minimum(count, SEQ))
    spread = jnp.where(valid[None], low_out[:, None, :], 0.0).reshape(1024, 256).astype(bf)
    loads[2].wait()
    loads[3].wait()
    low_in = jnp.dot(act_v[...], pin_v[...], preferred_element_type=f32).astype(bf)
    grads = jnp.dot(spread, low_in, preferred_element_type=f32).reshape(16, 8, 8, 128)
    for j in range(8):
        lg[:, :, pl.ds(j * 128, 128)] = grads[:, j].astype(bf)
    pl.semaphore_wait(barrier, 22)

    own_right = pltpu.make_async_copy(lg.at[pl.ds(2 * col, 2)], right.at[:, z, y, col], loc_sem.at[0])
    own_right.start()
    own_left = pltpu.make_async_copy(lg.at[row], left.at[z, y, col], loc_sem.at[1])
    own_left.start()
    stage_c, stage_r = [], []
    for k in (2, 6, 1, 7, 3, 5, 4):
        to = lax.rem(col + k, 8)
        stage_c.append(go(remote(lg.at[pl.ds(2 * to, 2)], right.at[:, z, y, col],
                                 c_send.at[k], c_recv.at[k], (row, to))))
    for k in range(1, 16):
        to = lax.rem(row + k, 16)
        stage_r.append(go(remote(lg.at[to], left.at[z, y, col], r_send.at[k], r_recv.at[k], (to, col))))
    loads[4].start()
    loads[5].start()

    yp, ym, zp, zm = at_y(1), at_y(3), at_z(1), at_z(3)
    xp = (row, lax.rem(x + 1, 4) * 2 + core)
    xm = (row, lax.rem(x + 3, 4) * 2 + core)
    partner = (row, x * 2 + 1 - core)
    lo5, hi5 = (lambda r: r.at[pl.ds(0, 4)]), (lambda r: r.at[pl.ds(4, 4)])
    a0 = Ring(go, lambda k: right.at[0, z, ymod(k)], lo5, hi5, ya_send, ya_recv, 0, yp, ym)
    a1 = Ring(go, lambda k: right.at[1, zmod(k), y], lo5, hi5, za_send, za_recv, 0, zp, zm)
    b0 = [Ring(go, lambda k, j=j: right.at[0, zmod(k), ymod(j)], lo5, hi5, za_send, za_recv, 4 + 4 * j, zp, zm)
          for j in range(4)]
    b1 = [Ring(go, lambda k, j=j: right.at[1, zmod(j), ymod(k)], lo5, hi5, ya_send, ya_recv, 4 + 4 * j, yp, ym)
          for j in range(4)]
    xr = Ring(go, lambda k: left.at[:, :, lax.rem(x + k, 4) * 2 + core], lambda r: r.at[pl.ds(0, 2)],
              lambda r: r.at[pl.ds(2, 2)], x_send, x_recv, 0, xp, xm)

    def to_partner(k):
        c = left.at[:, :, lax.rem(x + k, 4) * 2 + core]
        return go(remote(c, c, p_send.at[k], p_recv.at[k], partner))

    own_right.wait()
    own_left.wait()
    for c in stage_c:
        c.wait_recv()
    a0.start(); a1.start()
    b0[0].start(); b1[0].start()
    for c in stage_r:
        c.wait_recv()
    xr.start()
    pp = [to_partner(0)]
    a0.forward(); a1.forward()
    for j in (3, 1):
        b0[j].start(); b1[j].start()
    xr.forward()
    pp += [to_partner(3), to_partner(1)]
    b0[0].forward(); b1[0].forward()
    a0.finish(); a1.finish()
    b0[2].start(); b1[2].start()
    xr.finish()
    pp += [to_partner(2)]
    loads[4].wait()
    qt[...] = q[...].T.astype(bf)
    for c in pp:
        c.wait_recv()

    def left_of(h, j):
        block = left[:, ymod(j)] if h == 0 else left[zmod(j)]
        return block.astype(f32).reshape(256, 1024).T.astype(bf)

    def right_of(h, j):
        block = right[0, :, ymod(j)] if h == 0 else right[1, zmod(j)]
        return block.astype(f32).reshape(256, 1024).astype(bf)

    def multiply(h, j):
        add = jnp.dot(left_of(h, j), right_of(h, j), preferred_element_type=f32)
        acc[h] = add if j == 0 else acc[h] + add

    for j in (3, 1):
        b0[j].forward(); b1[j].forward()
    b0[0].finish(); b1[0].finish()
    multiply(0, 0)
    b0[2].forward(); b1[2].forward()
    multiply(1, 0)
    for j in (3, 1):
        b0[j].finish(); b1[j].finish()
        multiply(0, j); multiply(1, j)
    last = [left_of(h, 2) for h in range(2)]
    b0[2].finish(); b1[2].finish()
    loads[5].wait()

    lo, hi = pl.ds(0, 512), pl.ds(512, 512)

    def chunk(h, k):
        return part.at[0, :, ymod(k)] if h == 0 else part.at[1, zmod(k)]

    near = ((yp, ym), (zp, zm))
    far, plain, out = [], [], []
    for h in range(2):
        plus, minus = near[h]
        lanes = pl.ds(h * 1024, 1024)
        prod = acc[h] + jnp.dot(last[h], right_of(h, 2), preferred_element_type=f32)
        ri = lax.broadcasted_iota(jnp.int32, (1024, 1024), 0) + row * 1024
        ci = lax.broadcasted_iota(jnp.int32, (1024, 1024), 1) + (col * 2048 + h * 1024)
        g = decay_rate * old[:, lanes] + ((1.0 - decay_rate) / 1024) * prod
        g = g + jnp.where(ri == ci, damping, 0.0).astype(f32)
        acc[h] = g
        gb[h] = g.astype(bf)
        pt = jnp.dot(qt[...], gb[h], preferred_element_type=f32)
        part[h] = pt.astype(bf).reshape(4, 4, 16, 1024)
        far.append((go(remote(chunk(h, 2).at[:, :, lo], a_far.at[h, 0], s_a.at[h, 0], r_a.at[h, 0], plus)),
                    go(remote(chunk(h, 2).at[:, :, hi], a_far.at[h, 1], s_a.at[h, 1], r_a.at[h, 1], minus))))
        plain.append((go(remote(chunk(h, 1).at[:, :, hi], a_got.at[h, 0, 1], s_a.at[h, 2], r_a.at[h, 2], plus)),
                      go(remote(chunk(h, 3).at[:, :, lo], a_got.at[h, 1, 0], s_a.at[h, 3], r_a.at[h, 3], minus))))
        out.append(pltpu.make_async_copy(acc.at[h], new.at[:, lanes], out_sem.at[h]))
        out[h].start()
    joined = []
    for h in range(2):
        plus, minus = near[h]
        far[h][0].wait_recv()
        a_sum[h, 0] = (chunk(h, 1)[:, :, lo].astype(f32) + a_far[h, 0].astype(f32)).astype(bf)
        up = go(remote(a_sum.at[h, 0], a_got.at[h, 0, 0], s_a.at[h, 4], r_a.at[h, 4], plus))
        far[h][1].wait_recv()
        a_sum[h, 1] = (chunk(h, 3)[:, :, hi].astype(f32) + a_far[h, 1].astype(f32)).astype(bf)
        joined.append((up, go(remote(a_sum.at[h, 1], a_got.at[h, 1, 1], s_a.at[h, 5], r_a.at[h, 5], minus))))
    second = []
    for h in range(2):
        for c in plain[h] + joined[h]:
            c.wait_recv()
        for n, lanes in enumerate((lo, hi)):
            t = chunk(h, 0)[:, :, lanes].astype(f32) + a_got[h, 0, n].astype(f32) + a_got[h, 1, n].astype(f32)
            b_sum[h, :, :, lanes] = t.astype(bf)
        second.append([])
        for k in (1, 3, 2):
            to, dev = (zmod(k), at_z(k)) if h == 0 else (ymod(k), at_y(k))
            second[h].append(go(remote(b_sum.at[h, to], b_got.at[h, k - 1], s_b.at[h, k], r_b.at[h, k], dev)))

    lol, hil = (lambda r: r.at[:, lo]), (lambda r: r.at[:, hi])
    e0 = Ring(go, lambda k: wc.at[0, z, ymod(k)], lol, hil, ys, yr, 0, yp, ym)
    e1 = Ring(go, lambda k: wc.at[1, zmod(k), y], lol, hil, zs, zr, 0, zp, zm)
    f0 = [Ring(go, lambda k, j=j: wc.at[0, zmod(k), ymod(j)], lol, hil, zs, zr, 4 + 4 * j, zp, zm) for j in range(4)]
    f1 = [Ring(go, lambda k, j=j: wc.at[1, zmod(j), ymod(k)], lol, hil, ys, yr, 4 + 4 * j, yp, ym) for j in range(4)]
    half = y % 2
    mine = core == y // 2
    root = jnp.logical_and(mine, x == z)
    pieces = []

    def group(late, early):
        dz = jnp.where(half == 0, late, early)
        dy = jnp.where(half == 0, early, late)
        return zmod(dz), ymod(dy)

    def along(n, k):
        gz, gy = pieces[n]
        return remote(wc.at[half, gz, gy], wr.at[gz, gy], xs.at[n, k], xrecv.at[n], (row, lax.rem(x + k, 4) * 2 + core))

    def across(n, src):
        gz, gy = pieces[n]
        return remote(src.at[gz, gy], wr.at[gz, gy], ps.at[n], pr.at[n], partner)

    def publish(*which):
        first = len(pieces)
        pieces.extend(group(*w) for w in which)

        @pl.when(root)
        def _():
            for n in range(first, len(pieces)):
                for k in (1, 3, 2):
                    along(n, k).start()
                across(n, wc.at[half]).start()

    for h in range(2):
        for c in second[h]:
            c.wait_recv()
        t = b_sum[h, z if h == 0 else y].astype(f32)
        for k in range(3):
            t += b_got[h, k].astype(f32)
        wc[h, z, y] = t.astype(bf)
        (e0, e1)[h].start()
        (f0, f1)[h][0].start()
    publish((0, 0))
    e0.forward(); e1.forward()
    for j in (3, 1):
        f0[j].start(); f1[j].start()
    publish((0, 3), (0, 1))
    f0[0].forward(); f1[0].forward()
    e0.finish(); e1.finish()
    f0[2].start(); f1[2].start()
    publish((3, 0), (1, 0), (0, 2))
    for j in (3, 1, 2):
        f0[j].forward(); f1[j].forward()
        publish((3, j), (1, j))
    for j in (0, 3, 1, 2):
        f0[j].finish(); f1[j].finish()
        publish((2, j))

    @pl.when(root)
    def _():
        wr[...] = wc[half]
        for n in range(16):
            for k in (1, 3, 2):
                along(n, k).wait_send()
            across(n, wc.at[half]).wait_send()

    @pl.when(jnp.logical_and(mine, x != z))
    def _():
        for n in range(16):
            along(n, 1).wait_recv()
            across(n, wr).start()
        for n in range(16):
            across(n, wr).wait_send()

    @pl.when(jnp.logical_not(mine))
    def _():
        for n in range(16):
            across(n, wr).wait_recv()

    wrv = wr[...].reshape(256, 1024)
    v0 = jnp.dot(wrv, gb[0], preferred_element_type=f32) * wc[0].reshape(256, 1024).astype(f32)
    v1 = jnp.dot(wrv, gb[1], preferred_element_type=f32) * wc[1].reshape(256, 1024).astype(f32)
    curve = jnp.broadcast_to(jnp.sum(v0 + v1, axis=1, keepdims=True), (256, 128)).T
    w = wrv.astype(f32).T
    qv = q[...]
    once = jnp.where(col == 0, 1.0, 0.0).astype(f32)
    msg[0:1] = jnp.sum(qv * qv, axis=0, keepdims=True) * once
    msg[1:2] = jnp.sum(qv * w, axis=0, keepdims=True) * once
    msg[2:3] = jnp.sum(w * w, axis=0, keepdims=True) * once
    msg[3:4] = curve[3:4]
    cr = [go(remote(msg, got_r.at[k], s_r.at[k], r_r.at[k], (lax.rem(row + k, 16), col))) for k in range(1, 16)]
    t = msg[...]
    for k, c in enumerate(cr):
        c.wait_recv()
        t += got_r[k + 1]
    msg2[...] = t
    cc = [go(remote(msg2, got_c.at[k], s_c.at[k], r_c.at[k], (row, lax.rem(col + k, 8)))) for k in range(1, 8)]
    for k, c in enumerate(cc):
        c.wait_recv()
        t += got_c[k + 1]
    rr, qw, ww, gg = t[0:1], t[1:2], t[2:3], t[3:4]
    s1 = rr / qw
    new = s1 * s1 * ww - rr
    beta = new / rr
    up = 1.0 + beta
    s2 = new / (up * up * qw - 2.0 * up * s1 * ww + s1 * s1 * gg)
    x_out[...] = (s1 + s2 * up) * qv - (s2 * s1) * w
    for c in sends:
        c.wait_send()
    for c in out:
        c.wait()


def run(*args):
    dma = pltpu.SemaphoreType.DMA
    bf, f32 = jnp.bfloat16, jnp.float32
    vm = pltpu.VMEM
    hbm = pl.BlockSpec(memory_space=pl.ANY)
    return pl.pallas_call(
        kernel,
        out_shape=(jax.ShapeDtypeStruct((1024, 2048), f32), jax.ShapeDtypeStruct((1024, 256), f32)),
        in_specs=[hbm] * 4 + [pl.BlockSpec(memory_space=pltpu.SMEM)] + [hbm] * 2,
        out_specs=(hbm, pl.BlockSpec(memory_space=pltpu.VMEM)),
        scratch_shapes=[vm((256, 4096), bf), vm((256, 4096), bf), vm((4096, 128), bf), vm((4096, 128), bf),
                        vm((1024, 2048), f32), vm((1024, 256), f32), vm((16, 8, 1024), bf),
                        vm((4, 4, 8, 8, 1024), bf), vm((2, 4, 4, 8, 8, 1024), bf), vm((256, 1024), bf),
                        vm((2, 1024, 1024), f32), vm((2, 1024, 1024), bf), vm((2, 4, 4, 16, 1024), bf),
                        vm((2, 2, 4, 16, 512), bf), vm((2, 2, 2, 4, 16, 512), bf), vm((2, 2, 4, 16, 512), bf),
                        vm((2, 4, 16, 1024), bf), vm((2, 3, 16, 1024), bf), vm((2, 4, 4, 16, 1024), bf),
                        vm((4, 4, 16, 1024), bf),
                        vm((4, 256), f32), vm((16, 4, 256), f32), vm((4, 256), f32), vm((8, 4, 256), f32),
                        dma((6,)), dma((2,)), dma((2,)), dma((8,)), dma((8,)), dma((16,)), dma((16,)),
                        dma((20,)), dma((20,)), dma((20,)), dma((20,)), dma((4,)), dma((4,)), dma((4,)), dma((4,)),
                        dma((2, 6)), dma((2, 6)), dma((2, 4)), dma((2, 4)), dma((20,)), dma((20,)), dma((20,)), dma((20,)),
                        dma((16, 4)), dma((16,)), dma((16,)), dma((16,)), dma((16,)), dma((16,)), dma((8,)), dma((8,))],
        compiler_params=pltpu.CompilerParams(collective_id=0, has_side_effects=True, vmem_limit_bytes=62 * 1024 * 1024),
        name="influence",
    )(*args)


def solution(mesh):
    in_specs = (
        P(("row", "col"), None),
        P(("row", "col"), None),
        P(),
        P(),
        P(("row", "col")),
        P("row", "col"),
        P("row", None),
    )
    out_specs = (P("row", "col"), P("row", None))
    return jax.shard_map(run, mesh=mesh, in_specs=in_specs, out_specs=out_specs, check_vma=False)
```

time: 116 us -> 98.8 us (0.85)
  Pallas kernels: 107 us -> 89.1 us
  local copies, waits for them, and re-layouts: 3.95 us -> 8.95 us
  matrix products: 2.96 us -> 0 us
    pallas_call x3 -> x1, Pallas kernels: 107 us -> 89.1 us  [run(): pl.pallas_call(kernel, out_shape=(jax.ShapeDtypeStruct((1024, 2048), f32)...]
    unnamed x7 -> x4, local copies, waits for them, and re-layouts: 2.98 us -> 8.95 us
    dot_general x3 -> x0, matrix products: 2.96 us -> none  [the longest x1 1.92 us: shards(): jnp.dot(activations, proj_in, preferred_element_type=jnp.float32)]
where the time goes in v3:
time: 98.8 us; the launch traced here: 98.7 us
  Pallas kernels  89.1 us (90%)
  local copies, waits for them, and re-layouts  8.95 us (9%)
    pallas_call x1, Pallas kernels, run(): pl.pallas_call(kernel, out_shape=(jax.ShapeDtypeStruct((1024, 2048), f32)...  89.1 us
    unnamed x4, local copies, waits for them, and re-layouts  8.95 us

profile of v3, /device:TPU:1, one launch (start us, length us, event | category | flops | bytes accessed | tf_op | source)
XLA Modules:
  0.0 98.7 jit_solution(123846951493059763)
XLA Ops:
  0.6 89.1 %influence.1 = (f32[1024,2048]{1,0:T(8,128)}, f32[1024,256]{1,0:T(8,128)}) custom-call(bf16[256,4096]{1,0:T(8,128)(2,1)} %act.1, bf16[256,4096]{1,0:T(8,128)(2,1)} %og.1, bf16[4096,128]{1,0:T(8,128)(2,1)} %p_in.1, bf16[4096,128]{1,0:T(8,128)(2,1)} %p_out.1, s32[8]{0:T(128)} %lens.1, f32[1024,2048]{1,0:T(8,128)} %old_hbm.1, f32[1024,256]{1,0:T(8,128)} %q_hbm.1), custom_call_target="tpu_custom_call" | custom-call | tf_op jit(solution)/shard_map/influence/pallas_call | solution.py:359
  89.8 0.0 copy-start
  89.8 8.0 %copy.11 = f32[1024,2048]{1,0:T(8,128)} copy(f32[1024,2048]{1,0:T(8,128)} %get-tuple-element.4) | data formatting | bytes 16777216
  97.7 0.0 copy-done
  97.7 1.0 copy.12
Async XLA Ops:
  89.8 8.0 %copy-start = (f32[1024,256]{1,0:T(8,128)S(1)}, f32[1024,256]{1,0:T(8,128)}, u32[]{:S(2)}) copy-start(f32[1024,256]{1,0:T(8,128)} %get-tuple-element.5) | copy-start | bytes 3145732

commit v4 on v3

--- a/solution.py
+++ b/solution.py
@@ -51,10 +51,10 @@
     return barrier
 
 
-def kernel(act, og, p_in, p_out, lens, old_hbm, q_hbm, new, x_out,
-           act_v, og_v, pin_v, pout_v, old, q, lg, left, right, qt, acc, gb, part,
+def kernel(act, og, p_in, p_out, lens, old_hbm, q_hbm, acc, x_out,
+           act_v, og_v, pin_v, pout_v, old, q, lg, left, right, qt, gb, part,
            a_far, a_got, a_sum, b_sum, b_got, wc, wr, msg, got_r, msg2, got_c,
-           in_sem, out_sem, loc_sem, c_send, c_recv, r_send, r_recv, ya_send, ya_recv, za_send, za_recv,
+           in_sem, loc_sem, c_send, c_recv, r_send, r_recv, ya_send, ya_recv, za_send, za_recv,
            x_send, x_recv, p_send, p_recv,
            s_a, r_a, s_b, r_b, ys, yr, zs, zr, xs, xrecv, ps, pr, s_r, r_r, s_c, r_c):
     f32, bf = jnp.float32, jnp.bfloat16
@@ -197,7 +197,7 @@
         return part.at[0, :, ymod(k)] if h == 0 else part.at[1, zmod(k)]
 
     near = ((yp, ym), (zp, zm))
-    far, plain, out = [], [], []
+    far, plain = [], []
     for h in range(2):
         plus, minus = near[h]
         lanes = pl.ds(h * 1024, 1024)
@@ -214,8 +214,6 @@
                     go(remote(chunk(h, 2).at[:, :, hi], a_far.at[h, 1], s_a.at[h, 1], r_a.at[h, 1], minus))))
         plain.append((go(remote(chunk(h, 1).at[:, :, hi], a_got.at[h, 0, 1], s_a.at[h, 2], r_a.at[h, 2], plus)),
                       go(remote(chunk(h, 3).at[:, :, lo], a_got.at[h, 1, 0], s_a.at[h, 3], r_a.at[h, 3], minus))))
-        out.append(pltpu.make_async_copy(acc.at[h], new.at[:, lanes], out_sem.at[h]))
-        out[h].start()
     joined = []
     for h in range(2):
         plus, minus = near[h]
@@ -347,8 +345,6 @@
     x_out[...] = (s1 + s2 * up) * qv - (s2 * s1) * w
     for c in sends:
         c.wait_send()
-    for c in out:
-        c.wait()
 
 
 def run(*args):
@@ -358,24 +354,52 @@
     hbm = pl.BlockSpec(memory_space=pl.ANY)
     return pl.pallas_call(
         kernel,
-        out_shape=(jax.ShapeDtypeStruct((1024, 2048), f32), jax.ShapeDtypeStruct((1024, 256), f32)),
+        out_shape=(vm((2, 1024, 1024), f32), vm((1024, 256), f32)),
         in_specs=[hbm] * 4 + [pl.BlockSpec(memory_space=pltpu.SMEM)] + [hbm] * 2,
-        out_specs=(hbm, pl.BlockSpec(memory_space=pltpu.VMEM)),
+        out_specs=(pl.BlockSpec(memory_space=pltpu.VMEM),) * 2,
         scratch_shapes=[vm((256, 4096), bf), vm((256, 4096), bf), vm((4096, 128), bf), vm((4096, 128), bf),
                         vm((1024, 2048), f32), vm((1024, 256), f32), vm((16, 8, 1024), bf),
                         vm((4, 4, 8, 8, 1024), bf), vm((2, 4, 4, 8, 8, 1024), bf), vm((256, 1024), bf),
-                        vm((2, 1024, 1024), f32), vm((2, 1024, 1024), bf), vm((2, 4, 4, 16, 1024), bf),
+                        vm((2, 1024, 1024), bf), vm((2, 4, 4, 16, 1024), bf),
                         vm((2, 2, 4, 16, 512), bf), vm((2, 2, 2, 4, 16, 512), bf), vm((2, 2, 4, 16, 512), bf),
                         vm((2, 4, 16, 1024), bf), vm((2, 3, 16, 1024), bf), vm((2, 4, 4, 16, 1024), bf),
                         vm((4, 4, 16, 1024), bf),
                         vm((4, 256), f32), vm((16, 4, 256), f32), vm((4, 256), f32), vm((8, 4, 256), f32),
-                        dma((6,)), dma((2,)), dma((2,)), dma((8,)), dma((8,)), dma((16,)), dma((16,)),
+                        dma((6,)), dma((2,)), dma((8,)), dma((8,)), dma((16,)), dma((16,)),
                         dma((20,)), dma((20,)), dma((20,)), dma((20,)), dma((4,)), dma((4,)), dma((4,)), dma((4,)),
                         dma((2, 6)), dma((2, 6)), dma((2, 4)), dma((2, 4)), dma((20,)), dma((20,)), dma((20,)), dma((20,)),
                         dma((16, 4)), dma((16,)), dma((16,)), dma((16,)), dma((16,)), dma((16,)), dma((8,)), dma((8,))],
-        compiler_params=pltpu.CompilerParams(collective_id=0, has_side_effects=True, vmem_limit_bytes=62 * 1024 * 1024),
+        compiler_params=pltpu.CompilerParams(collective_id=0, has_side_effects=True, vmem_limit_bytes=44 * 1024 * 1024),
         name="influence",
     )(*args)
+
+
+def store_kernel(g, x, g_out, x_out, sem):
+    copies = [pltpu.make_async_copy(g.at[h, pl.ds(n * 256, 256)], g_out.at[pl.ds(n * 256, 256), pl.ds(h * 1024, 1024)],
+                                    sem.at[4 * h + n]) for h in range(2) for n in range(4)]
+    copies.append(pltpu.make_async_copy(x, x_out, sem.at[8]))
+    for c in copies:
+        c.start()
+    for c in copies:
+        c.wait()
+
+
+def store(g, x):
+    f32 = jnp.float32
+    inside, hbm = pl.BlockSpec(memory_space=pltpu.VMEM), pl.BlockSpec(memory_space=pltpu.HBM)
+    return pl.pallas_call(
+        store_kernel,
+        out_shape=(jax.ShapeDtypeStruct((1024, 2048), f32), jax.ShapeDtypeStruct((1024, 256), f32)),
+        in_specs=[inside] * 2,
+        out_specs=(hbm, hbm),
+        scratch_shapes=[pltpu.SemaphoreType.DMA((9,))],
+        compiler_params=pltpu.CompilerParams(vmem_limit_bytes=16 * 1024 * 1024),
+        name="store",
+    )(pltpu.with_memory_space_constraint(g, pltpu.VMEM), pltpu.with_memory_space_constraint(x, pltpu.VMEM))
+
+
+def whole(*args):
+    return store(*run(*args))
 
 
 def solution(mesh):
@@ -389,4 +413,4 @@
         P("row", None),
     )
     out_specs = (P("row", "col"), P("row", None))
-    return jax.shard_map(run, mesh=mesh, in_specs=in_specs, out_specs=out_specs, check_vma=False)
+    return jax.shard_map(whole, mesh=mesh, in_specs=in_specs, out_specs=out_specs, check_vma=False)

time: 98.8 us -> 93.5 us (0.946)
  local copies, waits for them, and re-layouts: 8.95 us -> 0.65 us
  Pallas kernels: 89.1 us -> 91.9 us
    unnamed x4 -> x2, local copies, waits for them, and re-layouts: 8.95 us -> 0.65 us
    pallas_call x1 -> x2, Pallas kernels: 89.1 us -> 91.9 us  [the longest x1 88.3 us: run(): pl.pallas_call(kernel, out_shape=(vm((2, 1024, 1024), f32), vm((1024, 256...]
where the time goes in v4:
time: 93.5 us; the launch traced here: 93.4 us
  Pallas kernels  91.9 us (98%)
    pallas_call x1, Pallas kernels, run(): pl.pallas_call(kernel, out_shape=(vm((2, 1024, 1024), f32), vm((1024, 256...  88.3 us
    pallas_call x1, Pallas kernels, store(): pl.pallas_call(store_kernel, out_shape=(jax.ShapeDtypeStruct((1024, 2048)...  3.69 us

profile of v4, /device:TPU:1, one launch (start us, length us, event | category | flops | bytes accessed | tf_op | source)
XLA Modules:
  0.0 93.4 jit_solution(3077269678548137962)
XLA Ops:
  0.6 0.0 copy-start
  0.6 0.6 copy-done
  1.3 88.3 %influence.1 = (f32[2,1024,1024]{2,1,0:T(8,128)S(1)}, f32[1024,256]{1,0:T(8,128)S(1)}) custom-call(bf16[256,4096]{1,0:T(8,128)(2,1)} %act.1, bf16[256,4096]{1,0:T(8,128)(2,1)} %og.1, bf16[4096,128]{1,0:T(8,128)(2,1)} %p_in.1, bf16[4096,128]{1,0:T(8,128)(2,1)} %p_out.1, s32[8]{0:T(128)S(1)} %copy-done, f32[1024,2048]{1,0:T(8,128)} %old_hbm.1, f32[1024,256]{1,0:T(8,128)} %q_hbm.1), custom_call_target="tpu_custom_call" | custom-call | tf_op jit(solution)/shard_map/influence/pallas_call | solution.py:355
  89.5 3.7 %store.1 = (f32[1024,2048]{1,0:T(8,128)}, f32[1024,256]{1,0:T(8,128)}) custom-call(f32[2,1024,1024]{2,1,0:T(8,128)S(1)} %get-tuple-element.4.g, f32[1024,256]{1,0:T(8,128)S(1)} %get-tuple-element.5.x), custom_call_target="tpu_custom_call" | custom-call | tf_op jit(solution)/shard_map/store/pallas_call | solution.py:390
Async XLA Ops:
  0.6 0.7 copy-start

commit v5 on v4

--- a/solution.py
+++ b/solution.py
@@ -52,7 +52,7 @@
 
 
 def kernel(act, og, p_in, p_out, lens, old_hbm, q_hbm, acc, x_out,
-           act_v, og_v, pin_v, pout_v, old, q, lg, left, right, qt, gb, part,
+           act_v, og_v, pin_v, pout_v, old, q, lg, left, right, qt, pt, last, y_last, gb, part,
            a_far, a_got, a_sum, b_sum, b_got, wc, wr, msg, got_r, msg2, got_c,
            in_sem, loc_sem, c_send, c_recv, r_send, r_recv, ya_send, ya_recv, za_send, za_recv,
            x_send, x_recv, p_send, p_recv,
@@ -166,6 +166,9 @@
     for c in pp:
         c.wait_recv()
 
+    lo, hi = pl.ds(0, 512), pl.ds(512, 512)
+    scale = (1.0 - decay_rate) / 1024
+
     def left_of(h, j):
         block = left[:, ymod(j)] if h == 0 else left[zmod(j)]
         return block.astype(f32).reshape(256, 1024).T.astype(bf)
@@ -175,45 +178,58 @@
         return block.astype(f32).reshape(256, 1024).astype(bf)
 
     def multiply(h, j):
-        add = jnp.dot(left_of(h, j), right_of(h, j), preferred_element_type=f32)
-        acc[h] = add if j == 0 else acc[h] + add
-
+        lt = left_of(h, j)
+        rt = right_of(h, j)
+        y16 = (scale * jnp.dot(qt[...], lt, preferred_element_type=f32)).astype(bf)
+        pt[h] += jnp.dot(y16, rt, preferred_element_type=f32)
+        add = scale * jnp.dot(lt, rt, preferred_element_type=f32)
+        acc[h] += add
+
+    def begin(h):
+        ri = lax.broadcasted_iota(jnp.int32, (1024, 1024), 0) + row * 1024
+        ci = lax.broadcasted_iota(jnp.int32, (1024, 1024), 1) + (col * 2048 + h * 1024)
+        g = decay_rate * old[:, pl.ds(h * 1024, 1024)] + jnp.where(ri == ci, damping, 0.0).astype(f32)
+        acc[h] = g
+        pt[h] = jnp.dot(qt[...], g.astype(bf), preferred_element_type=f32)
+
+    loads[5].wait()
     for j in (3, 1):
         b0[j].forward(); b1[j].forward()
-    b0[0].finish(); b1[0].finish()
+    begin(0)
+    b0[0].finish()
     multiply(0, 0)
     b0[2].forward(); b1[2].forward()
+    begin(1)
+    b1[0].finish()
     multiply(1, 0)
     for j in (3, 1):
         b0[j].finish(); b1[j].finish()
         multiply(0, j); multiply(1, j)
-    last = [left_of(h, 2) for h in range(2)]
-    b0[2].finish(); b1[2].finish()
-    loads[5].wait()
-
-    lo, hi = pl.ds(0, 512), pl.ds(512, 512)
+    for h in range(2):
+        lt = left_of(h, 2)
+        last[h] = lt
+        y_last[h] = (scale * jnp.dot(qt[...], lt, preferred_element_type=f32)).astype(bf)
 
     def chunk(h, k):
         return part.at[0, :, ymod(k)] if h == 0 else part.at[1, zmod(k)]
+
+    def tile(h):
+        g = acc[h] + scale * jnp.dot(last[h], right_of(h, 2), preferred_element_type=f32)
+        acc[h] = g
+        gb[h] = g.astype(bf)
 
     near = ((yp, ym), (zp, zm))
     far, plain = [], []
     for h in range(2):
+        (b0, b1)[h][2].finish()
         plus, minus = near[h]
-        lanes = pl.ds(h * 1024, 1024)
-        prod = acc[h] + jnp.dot(last[h], right_of(h, 2), preferred_element_type=f32)
-        ri = lax.broadcasted_iota(jnp.int32, (1024, 1024), 0) + row * 1024
-        ci = lax.broadcasted_iota(jnp.int32, (1024, 1024), 1) + (col * 2048 + h * 1024)
-        g = decay_rate * old[:, lanes] + ((1.0 - decay_rate) / 1024) * prod
-        g = g + jnp.where(ri == ci, damping, 0.0).astype(f32)
-        acc[h] = g
-        gb[h] = g.astype(bf)
-        pt = jnp.dot(qt[...], gb[h], preferred_element_type=f32)
-        part[h] = pt.astype(bf).reshape(4, 4, 16, 1024)
+        whole_pt = pt[h] + jnp.dot(y_last[h], right_of(h, 2), preferred_element_type=f32)
+        part[h] = whole_pt.astype(bf).reshape(4, 4, 16, 1024)
         far.append((go(remote(chunk(h, 2).at[:, :, lo], a_far.at[h, 0], s_a.at[h, 0], r_a.at[h, 0], plus)),
                     go(remote(chunk(h, 2).at[:, :, hi], a_far.at[h, 1], s_a.at[h, 1], r_a.at[h, 1], minus))))
         plain.append((go(remote(chunk(h, 1).at[:, :, hi], a_got.at[h, 0, 1], s_a.at[h, 2], r_a.at[h, 2], plus)),
                       go(remote(chunk(h, 3).at[:, :, lo], a_got.at[h, 1, 0], s_a.at[h, 3], r_a.at[h, 3], minus))))
+    tile(0)
     joined = []
     for h in range(2):
         plus, minus = near[h]
@@ -223,6 +239,7 @@
         far[h][1].wait_recv()
         a_sum[h, 1] = (chunk(h, 3)[:, :, hi].astype(f32) + a_far[h, 1].astype(f32)).astype(bf)
         joined.append((up, go(remote(a_sum.at[h, 1], a_got.at[h, 1, 1], s_a.at[h, 5], r_a.at[h, 5], minus))))
+    tile(1)
     second = []
     for h in range(2):
         for c in plain[h] + joined[h]:
@@ -360,6 +377,7 @@
         scratch_shapes=[vm((256, 4096), bf), vm((256, 4096), bf), vm((4096, 128), bf), vm((4096, 128), bf),
                         vm((1024, 2048), f32), vm((1024, 256), f32), vm((16, 8, 1024), bf),
                         vm((4, 4, 8, 8, 1024), bf), vm((2, 4, 4, 8, 8, 1024), bf), vm((256, 1024), bf),
+                        vm((2, 256, 1024), f32), vm((2, 1024, 256), bf), vm((2, 256, 256), bf),
                         vm((2, 1024, 1024), bf), vm((2, 4, 4, 16, 1024), bf),
                         vm((2, 2, 4, 16, 512), bf), vm((2, 2, 2, 4, 16, 512), bf), vm((2, 2, 4, 16, 512), bf),
                         vm((2, 4, 16, 1024), bf), vm((2, 3, 16, 1024), bf), vm((2, 4, 4, 16, 1024), bf),

time: 93.5 us -> 92.8 us (level)
  no operation moved by 1% of the time
where the time goes in v5:
time: 92.8 us; the launch traced here: 92.7 us
  Pallas kernels  91.2 us (98%)
    pallas_call x1, Pallas kernels, run(): pl.pallas_call(kernel, out_shape=(vm((2, 1024, 1024), f32), vm((1024, 256...  87.5 us
    pallas_call x1, Pallas kernels, store(): pl.pallas_call(store_kernel, out_shape=(jax.ShapeDtypeStruct((1024, 2048)...  3.69 us

profile of v5, /device:TPU:1, one launch (start us, length us, event | category | flops | bytes accessed | tf_op | source)
XLA Modules:
  0.0 92.7 jit_solution(10949404580132509108)
XLA Ops:
  0.6 0.0 copy-start
  0.6 0.6 copy-done
  1.3 87.5 %influence.1 = (f32[2,1024,1024]{2,1,0:T(8,128)S(1)}, f32[1024,256]{1,0:T(8,128)S(1)}) custom-call(bf16[256,4096]{1,0:T(8,128)(2,1)} %act.1, bf16[256,4096]{1,0:T(8,128)(2,1)} %og.1, bf16[4096,128]{1,0:T(8,128)(2,1)} %p_in.1, bf16[4096,128]{1,0:T(8,128)(2,1)} %p_out.1, s32[8]{0:T(128)S(1)} %copy-done, f32[1024,2048]{1,0:T(8,128)} %old_hbm.1, f32[1024,256]{1,0:T(8,128)} %q_hbm.1), custom_call_target="tpu_custom_call" | custom-call | tf_op jit(solution)/shard_map/influence/pallas_call | solution.py:372
  88.8 3.7 %store.1 = (f32[1024,2048]{1,0:T(8,128)}, f32[1024,256]{1,0:T(8,128)}) custom-call(f32[2,1024,1024]{2,1,0:T(8,128)S(1)} %get-tuple-element.4.g, f32[1024,256]{1,0:T(8,128)S(1)} %get-tuple-element.5.x), custom_call_target="tpu_custom_call" | custom-call | tf_op jit(solution)/shard_map/store/pallas_call | solution.py:408
Async XLA Ops:
  0.6 0.7 copy-start

commit v6 on v4

--- a/solution.py
+++ b/solution.py
@@ -52,11 +52,11 @@
 
 
 def kernel(act, og, p_in, p_out, lens, old_hbm, q_hbm, acc, x_out,
-           act_v, og_v, pin_v, pout_v, old, q, lg, left, right, qt, gb, part,
+           act_v, og_v, pin_v, pout_v, old, q, lg, left, right, qt, y_mine, y_got, proj, w_row, w_col, gb, part,
            a_far, a_got, a_sum, b_sum, b_got, wc, wr, msg, got_r, msg2, got_c,
            in_sem, loc_sem, c_send, c_recv, r_send, r_recv, ya_send, ya_recv, za_send, za_recv,
            x_send, x_recv, p_send, p_recv,
-           s_a, r_a, s_b, r_b, ys, yr, zs, zr, xs, xrecv, ps, pr, s_r, r_r, s_c, r_c):
+           s_y, r_y, s_z, r_z, s_a, r_a, s_b, r_b, ys, yr, zs, zr, xs, xrecv, ps, pr, s_r, r_r, s_c, r_c):
     f32, bf = jnp.float32, jnp.bfloat16
     row = lax.axis_index("row")
     col = lax.axis_index("col")
@@ -65,7 +65,7 @@
     barrier = greet(row, col)
     loads = [pltpu.make_async_copy(a, b, in_sem.at[n]) for n, (a, b) in enumerate(
         ((p_out, pout_v), (og, og_v), (p_in, pin_v), (act, act_v), (q_hbm, q), (old_hbm, old)))]
-    for c in loads[:4]:
+    for c in loads:
         c.start()
     sends = []
 
@@ -106,6 +106,21 @@
     grads = jnp.dot(spread, low_in, preferred_element_type=f32).reshape(16, 8, 8, 128)
     for j in range(8):
         lg[:, :, pl.ds(j * 128, 128)] = grads[:, j].astype(bf)
+    loads[4].wait()
+    q16 = q[...].T.astype(bf)
+    qt[...] = q16
+    scale = (1.0 - decay_rate) / 1024
+
+    def begin(h):
+        ri = lax.broadcasted_iota(jnp.int32, (1024, 1024), 0) + row * 1024
+        ci = lax.broadcasted_iota(jnp.int32, (1024, 1024), 1) + (col * 2048 + h * 1024)
+        g = decay_rate * old[:, pl.ds(h * 1024, 1024)] + jnp.where(ri == ci, damping, 0.0).astype(f32)
+        acc[h] = g
+        pt = jnp.dot(qt[...], g.astype(bf), preferred_element_type=f32)
+        part[h] = pt.astype(bf).reshape(4, 4, 16, 1024)
+
+    loads[5].wait()
+    begin(0)
     pl.semaphore_wait(barrier, 22)
 
     own_right = pltpu.make_async_copy(lg.at[pl.ds(2 * col, 2)], right.at[:, z, y, col], loc_sem.at[0])
@@ -120,9 +135,7 @@
     for k in range(1, 16):
         to = lax.rem(row + k, 16)
         stage_r.append(go(remote(lg.at[to], left.at[z, y, col], r_send.at[k], r_recv.at[k], (to, col))))
-    loads[4].start()
-    loads[5].start()
-
+    begin(1)
     yp, ym, zp, zm = at_y(1), at_y(3), at_z(1), at_z(3)
     xp = (row, lax.rem(x + 1, 4) * 2 + core)
     xm = (row, lax.rem(x + 3, 4) * 2 + core)
@@ -141,81 +154,22 @@
         c = left.at[:, :, lax.rem(x + k, 4) * 2 + core]
         return go(remote(c, c, p_send.at[k], p_recv.at[k], partner))
 
-    own_right.wait()
-    own_left.wait()
-    for c in stage_c:
-        c.wait_recv()
-    a0.start(); a1.start()
-    b0[0].start(); b1[0].start()
-    for c in stage_r:
-        c.wait_recv()
-    xr.start()
-    pp = [to_partner(0)]
-    a0.forward(); a1.forward()
-    for j in (3, 1):
-        b0[j].start(); b1[j].start()
-    xr.forward()
-    pp += [to_partner(3), to_partner(1)]
-    b0[0].forward(); b1[0].forward()
-    a0.finish(); a1.finish()
-    b0[2].start(); b1[2].start()
-    xr.finish()
-    pp += [to_partner(2)]
-    loads[4].wait()
-    qt[...] = q[...].T.astype(bf)
-    for c in pp:
-        c.wait_recv()
-
-    def left_of(h, j):
-        block = left[:, ymod(j)] if h == 0 else left[zmod(j)]
-        return block.astype(f32).reshape(256, 1024).T.astype(bf)
-
-    def right_of(h, j):
-        block = right[0, :, ymod(j)] if h == 0 else right[1, zmod(j)]
-        return block.astype(f32).reshape(256, 1024).astype(bf)
-
-    def multiply(h, j):
-        add = jnp.dot(left_of(h, j), right_of(h, j), preferred_element_type=f32)
-        acc[h] = add if j == 0 else acc[h] + add
-
-    for j in (3, 1):
-        b0[j].forward(); b1[j].forward()
-    b0[0].finish(); b1[0].finish()
-    multiply(0, 0)
-    b0[2].forward(); b1[2].forward()
-    multiply(1, 0)
-    for j in (3, 1):
-        b0[j].finish(); b1[j].finish()
-        multiply(0, j); multiply(1, j)
-    last = [left_of(h, 2) for h in range(2)]
-    b0[2].finish(); b1[2].finish()
-    loads[5].wait()
-
     lo, hi = pl.ds(0, 512), pl.ds(512, 512)
 
     def chunk(h, k):
         return part.at[0, :, ymod(k)] if h == 0 else part.at[1, zmod(k)]
 
     near = ((yp, ym), (zp, zm))
-    far, plain = [], []
-    for h in range(2):
+    far, plain, joined, second = [], [], [], []
+
+    def reduce_first(h):
         plus, minus = near[h]
-        lanes = pl.ds(h * 1024, 1024)
-        prod = acc[h] + jnp.dot(last[h], right_of(h, 2), preferred_element_type=f32)
-        ri = lax.broadcasted_iota(jnp.int32, (1024, 1024), 0) + row * 1024
-        ci = lax.broadcasted_iota(jnp.int32, (1024, 1024), 1) + (col * 2048 + h * 1024)
-        g = decay_rate * old[:, lanes] + ((1.0 - decay_rate) / 1024) * prod
-        g = g + jnp.where(ri == ci, damping, 0.0).astype(f32)
-        acc[h] = g
-        gb[h] = g.astype(bf)
-        pt = jnp.dot(qt[...], gb[h], preferred_element_type=f32)
-        part[h] = pt.astype(bf).reshape(4, 4, 16, 1024)
         far.append((go(remote(chunk(h, 2).at[:, :, lo], a_far.at[h, 0], s_a.at[h, 0], r_a.at[h, 0], plus)),
                     go(remote(chunk(h, 2).at[:, :, hi], a_far.at[h, 1], s_a.at[h, 1], r_a.at[h, 1], minus))))
         plain.append((go(remote(chunk(h, 1).at[:, :, hi], a_got.at[h, 0, 1], s_a.at[h, 2], r_a.at[h, 2], plus)),
                       go(remote(chunk(h, 3).at[:, :, lo], a_got.at[h, 1, 0], s_a.at[h, 3], r_a.at[h, 3], minus))))
-    joined = []
-    for h in range(2):
+
+    def reduce_join(h):
         plus, minus = near[h]
         far[h][0].wait_recv()
         a_sum[h, 0] = (chunk(h, 1)[:, :, lo].astype(f32) + a_far[h, 0].astype(f32)).astype(bf)
@@ -223,8 +177,8 @@
         far[h][1].wait_recv()
         a_sum[h, 1] = (chunk(h, 3)[:, :, hi].astype(f32) + a_far[h, 1].astype(f32)).astype(bf)
         joined.append((up, go(remote(a_sum.at[h, 1], a_got.at[h, 1, 1], s_a.at[h, 5], r_a.at[h, 5], minus))))
-    second = []
-    for h in range(2):
+
+    def reduce_second(h):
         for c in plain[h] + joined[h]:
             c.wait_recv()
         for n, lanes in enumerate((lo, hi)):
@@ -269,7 +223,7 @@
                     along(n, k).start()
                 across(n, wc.at[half]).start()
 
-    for h in range(2):
+    def gather_first(h):
         for c in second[h]:
             c.wait_recv()
         t = b_sum[h, z if h == 0 else y].astype(f32)
@@ -278,21 +232,109 @@
         wc[h, z, y] = t.astype(bf)
         (e0, e1)[h].start()
         (f0, f1)[h][0].start()
+
+    def left_of(h, j):
+        block = left[:, ymod(j)] if h == 0 else left[zmod(j)]
+        return block.astype(f32).reshape(256, 1024).T.astype(bf)
+
+    def right_of(h, j):
+        block = right[0, :, ymod(j)] if h == 0 else right[1, zmod(j)]
+        return block.astype(f32).reshape(256, 1024).astype(bf)
+
+    def multiply(h, j):
+        acc[h] += scale * jnp.dot(left_of(h, j), right_of(h, j), preferred_element_type=f32)
+
+    def examples_of(ref, c):
+        return ref[:, :, c].astype(f32).reshape(128, 1024)
+
+    def spread_of(ref):
+        total = jnp.zeros((256, 1024), f32)
+        for m in range(0, 8, 2):
+            pair = jnp.concatenate([proj[m + n].reshape(256, 128) for n in range(2)], axis=1)
+            rows = jnp.concatenate([examples_of(ref, m + n) for n in range(2)], axis=0).astype(bf)
+            total += jnp.dot(pair, rows, preferred_element_type=f32)
+        return total
+
+    reduce_first(0)
+    own_right.wait()
+    own_left.wait()
+    for c in stage_c:
+        c.wait_recv()
+    a0.start(); a1.start()
+    b0[0].start(); b1[0].start()
+    reduce_first(1)
+    for c in stage_r:
+        c.wait_recv()
+    xr.start()
+    pp = [to_partner(0)]
+    mine_t = examples_of(left, col).T.astype(bf)
+    y_mine[...] = (scale * jnp.dot(qt[...], mine_t, preferred_element_type=f32)).astype(bf).reshape(16, 16, 128)
+    ysum = [go(remote(y_mine.at[lax.rem(row + k, 16)], y_got.at[k], s_y.at[0, k], r_y.at[0, k],
+                      (lax.rem(row + k, 16), col))) for k in range(1, 16)]
+    reduce_join(0); reduce_join(1)
+    a0.forward(); a1.forward()
+    for j in (3, 1):
+        b0[j].start(); b1[j].start()
+    xr.forward()
+    pp += [to_partner(3), to_partner(1)]
+    reduce_second(0); reduce_second(1)
+    b0[0].forward(); b1[0].forward()
+    a0.finish(); a1.finish()
+    b0[2].start(); b1[2].start()
+    xr.finish()
+    pp += [to_partner(2)]
+    t = y_mine[row].astype(f32)
+    for k in range(1, 16):
+        ysum[k - 1].wait_recv()
+        t += y_got[k].astype(f32)
+    proj[col, row] = t.astype(bf)
+    yall = [go(remote(proj.at[col, row], proj.at[col, row], s_y.at[1, k], r_y.at[1, k],
+                      (lax.rem(row + k, 16), col))) for k in range(1, 16)]
+    gather_first(0); gather_first(1)
     publish((0, 0))
+    for j in (3, 1):
+        b0[j].forward(); b1[j].forward()
+    for c in yall:
+        c.wait_recv()
+    ycol = [go(remote(proj.at[col], proj.at[col], s_z.at[k], r_z.at[k], (row, lax.rem(col + k, 8))))
+            for k in range(1, 8)]
     e0.forward(); e1.forward()
     for j in (3, 1):
         f0[j].start(); f1[j].start()
     publish((0, 3), (0, 1))
+    for c in pp:
+        c.wait_recv()
+    b0[2].forward(); b1[2].forward()
+    b0[0].finish(); b1[0].finish()
+    multiply(0, 0)
     f0[0].forward(); f1[0].forward()
     e0.finish(); e1.finish()
     f0[2].start(); f1[2].start()
     publish((3, 0), (1, 0), (0, 2))
-    for j in (3, 1, 2):
-        f0[j].forward(); f1[j].forward()
-        publish((3, j), (1, j))
+    multiply(1, 0)
+    b0[3].finish(); b1[3].finish()
+    multiply(0, 3)
+    f0[3].forward(); f1[3].forward()
+    publish((3, 3), (1, 3))
+    multiply(1, 3)
+    f0[1].forward(); f1[1].forward()
+    publish((3, 1), (1, 1))
+    for c in ycol:
+        c.wait_recv()
+    w_row[...] = spread_of(left)
+    f0[2].forward(); f1[2].forward()
+    publish((3, 2), (1, 2))
+    b0[1].finish(); b1[1].finish()
+    multiply(0, 1)
     for j in (0, 3, 1, 2):
         f0[j].finish(); f1[j].finish()
         publish((2, j))
+    multiply(1, 1)
+    b0[2].finish(); b1[2].finish()
+    for h in range(2):
+        multiply(h, 2)
+        gb[h] = acc[h].astype(bf)
+        w_col[h] = spread_of(right.at[h]) + wc[h].reshape(256, 1024).astype(f32)
 
     @pl.when(root)
     def _():
@@ -315,11 +357,12 @@
         for n in range(16):
             across(n, wr).wait_recv()
 
-    wrv = wr[...].reshape(256, 1024)
-    v0 = jnp.dot(wrv, gb[0], preferred_element_type=f32) * wc[0].reshape(256, 1024).astype(f32)
-    v1 = jnp.dot(wrv, gb[1], preferred_element_type=f32) * wc[1].reshape(256, 1024).astype(f32)
+    wsum = wr[...].reshape(256, 1024).astype(f32) + w_row[...]
+    wrv = wsum.astype(bf)
+    v0 = jnp.dot(wrv, gb[0], preferred_element_type=f32) * w_col[0]
+    v1 = jnp.dot(wrv, gb[1], preferred_element_type=f32) * w_col[1]
     curve = jnp.broadcast_to(jnp.sum(v0 + v1, axis=1, keepdims=True), (256, 128)).T
-    w = wrv.astype(f32).T
+    w = wsum.T
     qv = q[...]
     once = jnp.where(col == 0, 1.0, 0.0).astype(f32)
     msg[0:1] = jnp.sum(qv * qv, axis=0, keepdims=True) * once
@@ -360,6 +403,8 @@
         scratch_shapes=[vm((256, 4096), bf), vm((256, 4096), bf), vm((4096, 128), bf), vm((4096, 128), bf),
                         vm((1024, 2048), f32), vm((1024, 256), f32), vm((16, 8, 1024), bf),
                         vm((4, 4, 8, 8, 1024), bf), vm((2, 4, 4, 8, 8, 1024), bf), vm((256, 1024), bf),
+                        vm((16, 16, 128), bf), vm((16, 16, 128), bf), vm((8, 16, 16, 128), bf), vm((256, 1024), f32),
+                        vm((2, 256, 1024), f32),
                         vm((2, 1024, 1024), bf), vm((2, 4, 4, 16, 1024), bf),
                         vm((2, 2, 4, 16, 512), bf), vm((2, 2, 2, 4, 16, 512), bf), vm((2, 2, 4, 16, 512), bf),
                         vm((2, 4, 16, 1024), bf), vm((2, 3, 16, 1024), bf), vm((2, 4, 4, 16, 1024), bf),
@@ -367,6 +412,7 @@
                         vm((4, 256), f32), vm((16, 4, 256), f32), vm((4, 256), f32), vm((8, 4, 256), f32),
                         dma((6,)), dma((2,)), dma((8,)), dma((8,)), dma((16,)), dma((16,)),
                         dma((20,)), dma((20,)), dma((20,)), dma((20,)), dma((4,)), dma((4,)), dma((4,)), dma((4,)),
+                        dma((2, 16)), dma((2, 16)), dma((8,)), dma((8,)),
                         dma((2, 6)), dma((2, 6)), dma((2, 4)), dma((2, 4)), dma((20,)), dma((20,)), dma((20,)), dma((20,)),
                         dma((16, 4)), dma((16,)), dma((16,)), dma((16,)), dma((16,)), dma((16,)), dma((8,)), dma((8,))],
         compiler_params=pltpu.CompilerParams(collective_id=0, has_side_effects=True, vmem_limit_bytes=44 * 1024 * 1024),

time: 93.5 us -> 82.4 us (0.88)
  Pallas kernels: 91.9 us -> 80.8 us
    pallas_call x1, Pallas kernels: 88.3 us -> 77.1 us  [run(): pl.pallas_call(kernel, out_shape=(vm((2, 1024, 1024), f32), vm((1024, 256...]
where the time goes in v6:
time: 82.4 us; the launch traced here: 82.3 us
  Pallas kernels  80.8 us (98%)
  between operations  0.83 us (1%)
    pallas_call x1, Pallas kernels, run(): pl.pallas_call(kernel, out_shape=(vm((2, 1024, 1024), f32), vm((1024, 256...  77.1 us
    pallas_call x1, Pallas kernels, store(): pl.pallas_call(store_kernel, out_shape=(jax.ShapeDtypeStruct((1024, 2048)...  3.69 us

profile of v6, /device:TPU:1, one launch (start us, length us, event | category | flops | bytes accessed | tf_op | source)
XLA Modules:
  0.0 82.3 jit_solution(324096535899346920)
XLA Ops:
  0.6 0.0 copy-start
  0.6 0.6 copy-done
  1.3 77.1 %influence.1 = (f32[2,1024,1024]{2,1,0:T(8,128)S(1)}, f32[1024,256]{1,0:T(8,128)S(1)}) custom-call(bf16[256,4096]{1,0:T(8,128)(2,1)} %act.1, bf16[256,4096]{1,0:T(8,128)(2,1)} %og.1, bf16[4096,128]{1,0:T(8,128)(2,1)} %p_in.1, bf16[4096,128]{1,0:T(8,128)(2,1)} %p_out.1, s32[8]{0:T(128)S(1)} %copy-done, f32[1024,2048]{1,0:T(8,128)} %old_hbm.1, f32[1024,256]{1,0:T(8,128)} %q_hbm.1), custom_call_target="tpu_custom_call" | custom-call | tf_op jit(solution)/shard_map/influence/pallas_call | solution.py:398
  78.4 3.7 %store.1 = (f32[1024,2048]{1,0:T(8,128)}, f32[1024,256]{1,0:T(8,128)}) custom-call(f32[2,1024,1024]{2,1,0:T(8,128)S(1)} %get-tuple-element.4.g, f32[1024,256]{1,0:T(8,128)S(1)} %get-tuple-element.5.x), custom_call_target="tpu_custom_call" | custom-call | tf_op jit(solution)/shard_map/store/pallas_call | solution.py:436
Async XLA Ops:
  0.6 0.7 copy-start

commit v7 on v6

--- a/solution.py
+++ b/solution.py
@@ -52,7 +52,7 @@
 
 
 def kernel(act, og, p_in, p_out, lens, old_hbm, q_hbm, acc, x_out,
-           act_v, og_v, pin_v, pout_v, old, q, lg, left, right, qt, y_mine, y_got, proj, w_row, w_col, gb, part,
+           act_v, og_v, pin_v, pout_v, old, q, lg, left, right, qt, y_mine, y_got, proj, w_row, w_col, last, gb, part,
            a_far, a_got, a_sum, b_sum, b_got, wc, wr, msg, got_r, msg2, got_c,
            in_sem, loc_sem, c_send, c_recv, r_send, r_recv, ya_send, ya_recv, za_send, za_recv,
            x_send, x_recv, p_send, p_recv,
@@ -65,7 +65,7 @@
     barrier = greet(row, col)
     loads = [pltpu.make_async_copy(a, b, in_sem.at[n]) for n, (a, b) in enumerate(
         ((p_out, pout_v), (og, og_v), (p_in, pin_v), (act, act_v), (q_hbm, q), (old_hbm, old)))]
-    for c in loads:
+    for c in loads[:4]:
         c.start()
     sends = []
 
@@ -92,6 +92,8 @@
 
     loads[0].wait()
     loads[1].wait()
+    loads[4].start()
+    loads[5].start()
     low_out = jnp.dot(og_v[...], pout_v[...], preferred_element_type=f32).astype(bf).astype(f32).T
     ex = lax.broadcasted_iota(jnp.int32, (8, 256), 0)
     slot = lax.broadcasted_iota(jnp.int32, (8, 256), 1) - SEQ * ex
@@ -123,19 +125,6 @@
     begin(0)
     pl.semaphore_wait(barrier, 22)
 
-    own_right = pltpu.make_async_copy(lg.at[pl.ds(2 * col, 2)], right.at[:, z, y, col], loc_sem.at[0])
-    own_right.start()
-    own_left = pltpu.make_async_copy(lg.at[row], left.at[z, y, col], loc_sem.at[1])
-    own_left.start()
-    stage_c, stage_r = [], []
-    for k in (2, 6, 1, 7, 3, 5, 4):
-        to = lax.rem(col + k, 8)
-        stage_c.append(go(remote(lg.at[pl.ds(2 * to, 2)], right.at[:, z, y, col],
-                                 c_send.at[k], c_recv.at[k], (row, to))))
-    for k in range(1, 16):
-        to = lax.rem(row + k, 16)
-        stage_r.append(go(remote(lg.at[to], left.at[z, y, col], r_send.at[k], r_recv.at[k], (to, col))))
-    begin(1)
     yp, ym, zp, zm = at_y(1), at_y(3), at_z(1), at_z(3)
     xp = (row, lax.rem(x + 1, 4) * 2 + core)
     xm = (row, lax.rem(x + 3, 4) * 2 + core)
@@ -255,14 +244,27 @@
             total += jnp.dot(pair, rows, preferred_element_type=f32)
         return total
 
+    own_right = pltpu.make_async_copy(lg.at[pl.ds(2 * col, 2)], right.at[:, z, y, col], loc_sem.at[0])
+    own_right.start()
+    own_left = pltpu.make_async_copy(lg.at[row], left.at[z, y, col], loc_sem.at[1])
+    own_left.start()
+    stage_c, stage_r = [], []
+    for k in (2, 6, 1, 7, 3, 5, 4):
+        to = lax.rem(col + k, 8)
+        stage_c.append(go(remote(lg.at[pl.ds(2 * to, 2)], right.at[:, z, y, col],
+                                 c_send.at[k], c_recv.at[k], (row, to))))
+    for k in range(1, 16):
+        to = lax.rem(row + k, 16)
+        stage_r.append(go(remote(lg.at[to], left.at[z, y, col], r_send.at[k], r_recv.at[k], (to, col))))
     reduce_first(0)
+    begin(1)
+    reduce_first(1)
     own_right.wait()
     own_left.wait()
     for c in stage_c:
         c.wait_recv()
     a0.start(); a1.start()
     b0[0].start(); b1[0].start()
-    reduce_first(1)
     for c in stage_r:
         c.wait_recv()
     xr.start()
@@ -330,10 +332,11 @@
         f0[j].finish(); f1[j].finish()
         publish((2, j))
     multiply(1, 1)
+    for h in range(2):
+        gb[h] = acc[h].astype(bf)
+        last[h] = left_of(h, 2)
     b0[2].finish(); b1[2].finish()
     for h in range(2):
-        multiply(h, 2)
-        gb[h] = acc[h].astype(bf)
         w_col[h] = spread_of(right.at[h]) + wc[h].reshape(256, 1024).astype(f32)
 
     @pl.when(root)
@@ -359,9 +362,12 @@
 
     wsum = wr[...].reshape(256, 1024).astype(f32) + w_row[...]
     wrv = wsum.astype(bf)
-    v0 = jnp.dot(wrv, gb[0], preferred_element_type=f32) * w_col[0]
-    v1 = jnp.dot(wrv, gb[1], preferred_element_type=f32) * w_col[1]
-    curve = jnp.broadcast_to(jnp.sum(v0 + v1, axis=1, keepdims=True), (256, 128)).T
+    v = jnp.zeros((256, 1024), f32)
+    for h in range(2):
+        u = (scale * jnp.dot(wrv, last[h], preferred_element_type=f32)).astype(bf)
+        v += (jnp.dot(wrv, gb[h], preferred_element_type=f32)
+              + jnp.dot(u, right_of(h, 2), preferred_element_type=f32)) * w_col[h]
+    curve = jnp.broadcast_to(jnp.sum(v, axis=1, keepdims=True), (256, 128)).T
     w = wsum.T
     qv = q[...]
     once = jnp.where(col == 0, 1.0, 0.0).astype(f32)
@@ -370,6 +376,8 @@
     msg[2:3] = jnp.sum(w * w, axis=0, keepdims=True) * once
     msg[3:4] = curve[3:4]
     cr = [go(remote(msg, got_r.at[k], s_r.at[k], r_r.at[k], (lax.rem(row + k, 16), col))) for k in range(1, 16)]
+    for h in range(2):
+        acc[h] += scale * jnp.dot(last[h], right_of(h, 2), preferred_element_type=f32)
     t = msg[...]
     for k, c in enumerate(cr):
         c.wait_recv()
@@ -404,7 +412,7 @@
                         vm((1024, 2048), f32), vm((1024, 256), f32), vm((16, 8, 1024), bf),
                         vm((4, 4, 8, 8, 1024), bf), vm((2, 4, 4, 8, 8, 1024), bf), vm((256, 1024), bf),
                         vm((16, 16, 128), bf), vm((16, 16, 128), bf), vm((8, 16, 16, 128), bf), vm((256, 1024), f32),
-                        vm((2, 256, 1024), f32),
+                        vm((2, 256, 1024), f32), vm((2, 1024, 256), bf),
                         vm((2, 1024, 1024), bf), vm((2, 4, 4, 16, 1024), bf),
                         vm((2, 2, 4, 16, 512), bf), vm((2, 2, 2, 4, 16, 512), bf), vm((2, 2, 4, 16, 512), bf),
                         vm((2, 4, 16, 1024), bf), vm((2, 3, 16, 1024), bf), vm((2, 4, 4, 16, 1024), bf),

time: 82.4 us -> 80.9 us (0.982)
  Pallas kernels: 80.8 us -> 79.3 us
    pallas_call x1, Pallas kernels: 77.1 us -> 75.6 us  [run(): pl.pallas_call(kernel, out_shape=(vm((2, 1024, 1024), f32), vm((1024, 256...]
where the time goes in v7:
time: 80.9 us; the launch traced here: 80.8 us
  Pallas kernels  79.3 us (98%)
  between operations  0.81 us (1%)
    pallas_call x1, Pallas kernels, run(): pl.pallas_call(kernel, out_shape=(vm((2, 1024, 1024), f32), vm((1024, 256...  75.6 us
    pallas_call x1, Pallas kernels, store(): pl.pallas_call(store_kernel, out_shape=(jax.ShapeDtypeStruct((1024, 2048)...  3.69 us

profile of v7, /device:TPU:1, one launch (start us, length us, event | category | flops | bytes accessed | tf_op | source)
XLA Modules:
  0.0 80.8 jit_solution(12794299852568134808)
XLA Ops:
  0.6 0.0 copy-start
  0.6 0.6 copy-done
  1.3 75.6 %influence.1 = (f32[2,1024,1024]{2,1,0:T(8,128)S(1)}, f32[1024,256]{1,0:T(8,128)S(1)}) custom-call(bf16[256,4096]{1,0:T(8,128)(2,1)} %act.1, bf16[256,4096]{1,0:T(8,128)(2,1)} %og.1, bf16[4096,128]{1,0:T(8,128)(2,1)} %p_in.1, bf16[4096,128]{1,0:T(8,128)(2,1)} %p_out.1, s32[8]{0:T(128)S(1)} %copy-done, f32[1024,2048]{1,0:T(8,128)} %old_hbm.1, f32[1024,256]{1,0:T(8,128)} %q_hbm.1), custom_call_target="tpu_custom_call" | custom-call | tf_op jit(solution)/shard_map/influence/pallas_call | solution.py:406
  76.9 3.7 %store.1 = (f32[1024,2048]{1,0:T(8,128)}, f32[1024,256]{1,0:T(8,128)}) custom-call(f32[2,1024,1024]{2,1,0:T(8,128)S(1)} %get-tuple-element.4.g, f32[1024,256]{1,0:T(8,128)S(1)} %get-tuple-element.5.x), custom_call_target="tpu_custom_call" | custom-call | tf_op jit(solution)/shard_map/store/pallas_call | solution.py:444
Async XLA Ops:
  0.6 0.7 copy-start

commit v8 on v7

--- a/solution.py
+++ b/solution.py
@@ -275,14 +275,13 @@
                       (lax.rem(row + k, 16), col))) for k in range(1, 16)]
     reduce_join(0); reduce_join(1)
     a0.forward(); a1.forward()
-    for j in (3, 1):
-        b0[j].start(); b1[j].start()
+    b0[3].start(); b1[3].start()
     xr.forward()
     pp += [to_partner(3), to_partner(1)]
     reduce_second(0); reduce_second(1)
     b0[0].forward(); b1[0].forward()
+    b0[1].start(); b1[1].start()
     a0.finish(); a1.finish()
-    b0[2].start(); b1[2].start()
     xr.finish()
     pp += [to_partner(2)]
     t = y_mine[row].astype(f32)
@@ -292,46 +291,47 @@
     proj[col, row] = t.astype(bf)
     yall = [go(remote(proj.at[col, row], proj.at[col, row], s_y.at[1, k], r_y.at[1, k],
                       (lax.rem(row + k, 16), col))) for k in range(1, 16)]
+    b0[3].forward(); b1[3].forward()
+    b0[2].start(); b1[2].start()
     gather_first(0); gather_first(1)
     publish((0, 0))
-    for j in (3, 1):
-        b0[j].forward(); b1[j].forward()
+    for c in pp:
+        c.wait_recv()
+    b0[0].finish(); b1[0].finish()
+    multiply(0, 0)
     for c in yall:
         c.wait_recv()
     ycol = [go(remote(proj.at[col], proj.at[col], s_z.at[k], r_z.at[k], (row, lax.rem(col + k, 8))))
             for k in range(1, 8)]
+    b0[1].forward(); b1[1].forward()
+    multiply(1, 0)
     e0.forward(); e1.forward()
     for j in (3, 1):
         f0[j].start(); f1[j].start()
     publish((0, 3), (0, 1))
-    for c in pp:
-        c.wait_recv()
-    b0[2].forward(); b1[2].forward()
-    b0[0].finish(); b1[0].finish()
-    multiply(0, 0)
+    b0[3].finish(); b1[3].finish()
+    multiply(0, 3)
     f0[0].forward(); f1[0].forward()
     e0.finish(); e1.finish()
     f0[2].start(); f1[2].start()
     publish((3, 0), (1, 0), (0, 2))
-    multiply(1, 0)
-    b0[3].finish(); b1[3].finish()
-    multiply(0, 3)
+    b0[2].forward(); b1[2].forward()
+    multiply(1, 3)
     f0[3].forward(); f1[3].forward()
     publish((3, 3), (1, 3))
-    multiply(1, 3)
+    for c in ycol:
+        c.wait_recv()
+    w_row[...] = spread_of(left)
     f0[1].forward(); f1[1].forward()
     publish((3, 1), (1, 1))
-    for c in ycol:
-        c.wait_recv()
-    w_row[...] = spread_of(left)
+    b0[1].finish(); b1[1].finish()
+    multiply(0, 1)
     f0[2].forward(); f1[2].forward()
     publish((3, 2), (1, 2))
-    b0[1].finish(); b1[1].finish()
-    multiply(0, 1)
+    multiply(1, 1)
     for j in (0, 3, 1, 2):
         f0[j].finish(); f1[j].finish()
         publish((2, j))
-    multiply(1, 1)
     for h in range(2):
         gb[h] = acc[h].astype(bf)
         last[h] = left_of(h, 2)

time: 80.9 us -> 80.6 us (level)
  no operation moved by 1% of the time
where the time goes in v8:
time: 80.6 us; the launch traced here: 80.5 us
  Pallas kernels  79.1 us (98%)
  between operations  0.81 us (1%)
    pallas_call x1, Pallas kernels, run(): pl.pallas_call(kernel, out_shape=(vm((2, 1024, 1024), f32), vm((1024, 256...  75.4 us
    pallas_call x1, Pallas kernels, store(): pl.pallas_call(store_kernel, out_shape=(jax.ShapeDtypeStruct((1024, 2048)...  3.69 us

profile of v8, /device:TPU:1, one launch (start us, length us, event | category | flops | bytes accessed | tf_op | source)
XLA Modules:
  0.0 80.5 jit_solution(15042495921113369146)
XLA Ops:
  0.6 0.0 copy-start
  0.6 0.6 copy-done
  1.3 75.4 %influence.1 = (f32[2,1024,1024]{2,1,0:T(8,128)S(1)}, f32[1024,256]{1,0:T(8,128)S(1)}) custom-call(bf16[256,4096]{1,0:T(8,128)(2,1)} %act.1, bf16[256,4096]{1,0:T(8,128)(2,1)} %og.1, bf16[4096,128]{1,0:T(8,128)(2,1)} %p_in.1, bf16[4096,128]{1,0:T(8,128)(2,1)} %p_out.1, s32[8]{0:T(128)S(1)} %copy-done, f32[1024,2048]{1,0:T(8,128)} %old_hbm.1, f32[1024,256]{1,0:T(8,128)} %q_hbm.1), custom_call_target="tpu_custom_call" | custom-call | tf_op jit(solution)/shard_map/influence/pallas_call | solution.py:406
  76.7 3.7 %store.1 = (f32[1024,2048]{1,0:T(8,128)}, f32[1024,256]{1,0:T(8,128)}) custom-call(f32[2,1024,1024]{2,1,0:T(8,128)S(1)} %get-tuple-element.4.g, f32[1024,256]{1,0:T(8,128)S(1)} %get-tuple-element.5.x), custom_call_target="tpu_custom_call" | custom-call | tf_op jit(solution)/shard_map/store/pallas_call | solution.py:444
Async XLA Ops:
  0.6 0.7 copy-start

commit v9 on v8

--- a/solution.py
+++ b/solution.py
@@ -185,7 +185,8 @@
     f1 = [Ring(go, lambda k, j=j: wc.at[1, zmod(j), ymod(k)], lol, hil, ys, yr, 4 + 4 * j, yp, ym) for j in range(4)]
     half = y % 2
     mine = core == y // 2
-    root = jnp.logical_and(mine, x == z)
+    away = lax.rem(x - z + 4, 4)
+    root = jnp.logical_and(mine, away == 0)
     pieces = []
 
     def group(late, early):
@@ -201,6 +202,21 @@
         gz, gy = pieces[n]
         return remote(src.at[gz, gy], wr.at[gz, gy], ps.at[n], pr.at[n], partner)
 
+    def relay(n, k):
+        gz, gy = pieces[n]
+        return remote(wr.at[gz, gy], wr.at[gz, gy], xs.at[n, k], xrecv.at[n], (row, lax.rem(x + k, 4) * 2 + core))
+
+    def pass_on(first, stop):
+        for place, k in ((1, 1), (3, 3)):
+            @pl.when(jnp.logical_and(mine, away == place))
+            def _(place=place, k=k):
+                for n in range(first, stop):
+                    if n % 2 == place // 2:
+                        relay(n, k).wait_recv()
+                        relay(n, k).start()
+
+    done = [0]
+
     def publish(*which):
         first = len(pieces)
         pieces.extend(group(*w) for w in which)
@@ -208,9 +224,11 @@
         @pl.when(root)
         def _():
             for n in range(first, len(pieces)):
-                for k in (1, 3, 2):
+                for k in (1, 3):
                     along(n, k).start()
                 across(n, wc.at[half]).start()
+        pass_on(done[0], first)
+        done[0] = first
 
     def gather_first(h):
         for c in second[h]:
@@ -273,6 +291,13 @@
     y_mine[...] = (scale * jnp.dot(qt[...], mine_t, preferred_element_type=f32)).astype(bf).reshape(16, 16, 128)
     ysum = [go(remote(y_mine.at[lax.rem(row + k, 16)], y_got.at[k], s_y.at[0, k], r_y.at[0, k],
                       (lax.rem(row + k, 16), col))) for k in range(1, 16)]
+    yr_ = Ring(go, lambda k: proj.at[lax.rem(x + k, 4) * 2 + core], lambda r: r.at[pl.ds(0, 8)],
+               lambda r: r.at[pl.ds(8, 8)], s_z, r_z, 0, xp, xm)
+
+    def y_partner(k):
+        c = proj.at[lax.rem(x + k, 4) * 2 + core]
+        return go(remote(c, c, s_z.at[4 + k], r_z.at[4 + k], partner))
+
     reduce_join(0); reduce_join(1)
     a0.forward(); a1.forward()
     b0[3].start(); b1[3].start()
@@ -301,8 +326,8 @@
     multiply(0, 0)
     for c in yall:
         c.wait_recv()
-    ycol = [go(remote(proj.at[col], proj.at[col], s_z.at[k], r_z.at[k], (row, lax.rem(col + k, 8))))
-            for k in range(1, 8)]
+    yr_.start()
+    ycol = [y_partner(0)]
     b0[1].forward(); b1[1].forward()
     multiply(1, 0)
     e0.forward(); e1.forward()
@@ -316,9 +341,13 @@
     f0[2].start(); f1[2].start()
     publish((3, 0), (1, 0), (0, 2))
     b0[2].forward(); b1[2].forward()
+    yr_.forward()
+    ycol += [y_partner(3), y_partner(1)]
     multiply(1, 3)
     f0[3].forward(); f1[3].forward()
     publish((3, 3), (1, 3))
+    yr_.finish()
+    ycol += [y_partner(2)]
     for c in ycol:
         c.wait_recv()
     w_row[...] = spread_of(left)
@@ -343,17 +372,22 @@
     def _():
         wr[...] = wc[half]
         for n in range(16):
-            for k in (1, 3, 2):
+            for k in (1, 3):
                 along(n, k).wait_send()
             across(n, wc.at[half]).wait_send()
 
-    @pl.when(jnp.logical_and(mine, x != z))
-    def _():
-        for n in range(16):
-            along(n, 1).wait_recv()
-            across(n, wr).start()
-        for n in range(16):
-            across(n, wr).wait_send()
+    pass_on(done[0], 16)
+    for place in (1, 2, 3):
+        @pl.when(jnp.logical_and(mine, away == place))
+        def _(place=place):
+            for n in range(16):
+                if place == 2 or n % 2 != place // 2:
+                    along(n, 1).wait_recv()
+                across(n, wr).start()
+            for n in range(16):
+                if place != 2 and n % 2 == place // 2:
+                    relay(n, place).wait_send()
+                across(n, wr).wait_send()
 
     @pl.when(jnp.logical_not(mine))
     def _():

time: 80.6 us -> 84.3 us (1.046)
  Pallas kernels: 79.1 us -> 82.8 us
    pallas_call x1, Pallas kernels: 75.4 us -> 79.1 us  [run(): pl.pallas_call(kernel, out_shape=(vm((2, 1024, 1024), f32), vm((1024, 256...]
where the time goes in v9:
time: 84.3 us; the launch traced here: 84.2 us
  Pallas kernels  82.8 us (98%)
    pallas_call x1, Pallas kernels, run(): pl.pallas_call(kernel, out_shape=(vm((2, 1024, 1024), f32), vm((1024, 256...  79.1 us
    pallas_call x1, Pallas kernels, store(): pl.pallas_call(store_kernel, out_shape=(jax.ShapeDtypeStruct((1024, 2048)...  3.69 us

profile of v9, /device:TPU:1, one launch (start us, length us, event | category | flops | bytes accessed | tf_op | source)
XLA Modules:
  0.0 84.2 jit_solution(18435904318421476117)
XLA Ops:
  0.6 0.0 copy-start
  0.6 0.6 copy-done
  1.3 79.1 %influence.1 = (f32[2,1024,1024]{2,1,0:T(8,128)S(1)}, f32[1024,256]{1,0:T(8,128)S(1)}) custom-call(bf16[256,4096]{1,0:T(8,128)(2,1)} %act.1, bf16[256,4096]{1,0:T(8,128)(2,1)} %og.1, bf16[4096,128]{1,0:T(8,128)(2,1)} %p_in.1, bf16[4096,128]{1,0:T(8,128)(2,1)} %p_out.1, s32[8]{0:T(128)S(1)} %copy-done, f32[1024,2048]{1,0:T(8,128)} %old_hbm.1, f32[1024,256]{1,0:T(8,128)} %q_hbm.1), custom_call_target="tpu_custom_call" | custom-call | tf_op jit(solution)/shard_map/influence/pallas_call | solution.py:440
  80.4 3.7 %store.1 = (f32[1024,2048]{1,0:T(8,128)}, f32[1024,256]{1,0:T(8,128)}) custom-call(f32[2,1024,1024]{2,1,0:T(8,128)S(1)} %get-tuple-element.4.g, f32[1024,256]{1,0:T(8,128)S(1)} %get-tuple-element.5.x), custom_call_target="tpu_custom_call" | custom-call | tf_op jit(solution)/shard_map/store/pallas_call | solution.py:478
Async XLA Ops:
  0.6 0.7 copy-start

commit v10 on v7

--- a/solution.py
+++ b/solution.py
@@ -273,6 +273,10 @@
     y_mine[...] = (scale * jnp.dot(qt[...], mine_t, preferred_element_type=f32)).astype(bf).reshape(16, 16, 128)
     ysum = [go(remote(y_mine.at[lax.rem(row + k, 16)], y_got.at[k], s_y.at[0, k], r_y.at[0, k],
                       (lax.rem(row + k, 16), col))) for k in range(1, 16)]
+    def y_partner(k):
+        c = proj.at[lax.rem(x + k, 4) * 2 + core]
+        return go(remote(c, c, s_z.at[4 + k], r_z.at[4 + k], partner))
+
     reduce_join(0); reduce_join(1)
     a0.forward(); a1.forward()
     for j in (3, 1):
@@ -298,8 +302,9 @@
         b0[j].forward(); b1[j].forward()
     for c in yall:
         c.wait_recv()
-    ycol = [go(remote(proj.at[col], proj.at[col], s_z.at[k], r_z.at[k], (row, lax.rem(col + k, 8))))
-            for k in range(1, 8)]
+    ycol = [go(remote(proj.at[col], proj.at[col], s_z.at[k], r_z.at[k], (row, lax.rem(x + k, 4) * 2 + core)))
+            for k in (1, 3, 2)]
+    ypart = [y_partner(0)]
     e0.forward(); e1.forward()
     for j in (3, 1):
         f0[j].start(); f1[j].start()
@@ -321,7 +326,10 @@
     multiply(1, 3)
     f0[1].forward(); f1[1].forward()
     publish((3, 1), (1, 1))
-    for c in ycol:
+    for c, k in zip(ycol, (3, 1, 2)):
+        c.wait_recv()
+        ypart.append(y_partner(k))
+    for c in ypart:
         c.wait_recv()
     w_row[...] = spread_of(left)
     f0[2].forward(); f1[2].forward()

time: 80.9 us -> 79.6 us (0.984)
  Pallas kernels: 79.3 us -> 78 us
    pallas_call x1, Pallas kernels: 75.6 us -> 74.3 us  [run(): pl.pallas_call(kernel, out_shape=(vm((2, 1024, 1024), f32), vm((1024, 256...]
where the time goes in v10:
time: 79.6 us; the launch traced here: 79.4 us
  Pallas kernels  78 us (98%)
  between operations  0.81 us (1%)
    pallas_call x1, Pallas kernels, run(): pl.pallas_call(kernel, out_shape=(vm((2, 1024, 1024), f32), vm((1024, 256...  74.3 us
    pallas_call x1, Pallas kernels, store(): pl.pallas_call(store_kernel, out_shape=(jax.ShapeDtypeStruct((1024, 2048)...  3.69 us

profile of v10, /device:TPU:1, one launch (start us, length us, event | category | flops | bytes accessed | tf_op | source)
XLA Modules:
  0.0 79.4 jit_solution(8636133937940073417)
XLA Ops:
  0.6 0.0 copy-start
  0.6 0.6 copy-done
  1.3 74.3 %influence.1 = (f32[2,1024,1024]{2,1,0:T(8,128)S(1)}, f32[1024,256]{1,0:T(8,128)S(1)}) custom-call(bf16[256,4096]{1,0:T(8,128)(2,1)} %act.1, bf16[256,4096]{1,0:T(8,128)(2,1)} %og.1, bf16[4096,128]{1,0:T(8,128)(2,1)} %p_in.1, bf16[4096,128]{1,0:T(8,128)(2,1)} %p_out.1, s32[8]{0:T(128)S(1)} %copy-done, f32[1024,2048]{1,0:T(8,128)} %old_hbm.1, f32[1024,256]{1,0:T(8,128)} %q_hbm.1), custom_call_target="tpu_custom_call" | custom-call | tf_op jit(solution)/shard_map/influence/pallas_call | solution.py:414
  75.6 3.7 %store.1 = (f32[1024,2048]{1,0:T(8,128)}, f32[1024,256]{1,0:T(8,128)}) custom-call(f32[2,1024,1024]{2,1,0:T(8,128)S(1)} %get-tuple-element.4.g, f32[1024,256]{1,0:T(8,128)S(1)} %get-tuple-element.5.x), custom_call_target="tpu_custom_call" | custom-call | tf_op jit(solution)/shard_map/store/pallas_call | solution.py:452
Async XLA Ops:
  0.6 0.7 copy-start
